TPU v7x, 512 devices: a whole 4x8x8 slice. The times are simulated.
512 devices in a mesh: seq: 16 (over z, core), head: 32 (over x, y).
Axes of the slice: x: 4, y: 8, z: 8, core: 2. Of those that a mesh axis runs over, the one named last changes fastest.
Arguments:
- x_in: bfloat16 [16384, 16384], P('seq', 'head'), may hold values from -40 to 40
- z_gate: bfloat16 [16384, 16384], P('seq', 'head'), may hold values from -6 to 6
- b_input: bfloat16 [16384, 8, 128], P('seq'), may hold values from -2 to 2
- c_input: bfloat16 [16384, 8, 128], P('seq'), may hold values from -2 to 2
- dt_raw: float32 [128, 16384], P('head', 'seq'), may hold values from -5 to 5462
- a_log: float32 [128], P('head'), may hold values from -20 to 0
- d_skip: float32 [128], P('head'), may hold values from 0.5 to 2
- norm_gain: float32 [16384], P('head'), may hold values from 0.25 to 1.75
- doc_lengths: int32 [6], replicated, may hold values from 1 to 5461, 16384 in all
- doc_lang: int32 [6], replicated, may hold values from 0 to 3
- adapt_down: bfloat16 [4, 16384, 128], P(None, 'head'), may hold values from -0.046875 to 0.046875
- adapt_up: bfloat16 [4, 128, 16384], P(None, None, 'head'), may hold values from -0.5 to 0.5
Outputs:
- adapted: bfloat16 [16384, 16384], P('seq', 'head')
Inputs may be any that keep to these rules, and one draw needn't show every extreme that they name: `doc_lengths`: the lengths sum to 16384; the longest document has exactly 5461 tokens.
All inputs are finite; a program needn't handle non-finite values.
Results may differ from a plain program's by a relative error of at most 0.0075.
Values may be sent and summed in bfloat16 or wider, within the bound.
A program may use at most 64 MiB of HBM per device.

v0:
```python
import jax
import jax.numpy as jnp
from jax import lax
from jax.sharding import PartitionSpec as P

SPACE_HEADS = 128
HEAD_DIM = 128
GROUPS = 8


highest = lax.Precision.HIGHEST


def prefix(x, axis, combine, identity):
    peers, mine = (lax.axis_size(axis), lax.axis_index(axis))
    everything = jax.tree.map(lambda part: lax.all_gather(part, axis), x)
    start = jax.tree.map(
        lambda part, zero: jnp.broadcast_to(jnp.asarray(zero, part.dtype), part.shape), x, identity
    )

    def hop(k, before):
        reached = k < mine
        new = combine(before, jax.tree.map(lambda part: part[k], everything))
        return jax.tree.map(lambda a, b: jnp.where(reached, a, b), new, before)

    return lax.fori_loop(0, peers, hop, start)


def doc_tables(doc_lengths, doc_lang, token_positions, lang_count):
    doc_ends = jnp.cumsum(doc_lengths)
    doc_start = doc_ends - doc_lengths
    doc_index = (
        jnp.sum((token_positions[:, None] >= doc_start[None, :]).astype(jnp.int32), axis=1) - 1
    )
    is_first = jnp.sum((token_positions[:, None] == doc_start[None, :]).astype(jnp.int32), axis=1)
    doc_hot = (
        doc_index[:, None] == jnp.arange(doc_lengths.shape[0], dtype=jnp.int32)[None, :]
    ).astype(jnp.int32)
    lang_index = jnp.sum(doc_hot * doc_lang[None, :], axis=1)
    lang_hot = lang_index[:, None] == jnp.arange(lang_count, dtype=jnp.int32)[None, :]
    return (doc_index, is_first, lang_hot)


def block_scan(x_vals, step_dt, log_decay, b_vals, c_vals, doc_index, is_first):
    head_count, length, head_width = x_vals.shape
    states = b_vals.shape[1]
    block_len = min(128, length)
    block_count = length // block_len
    x_blocks = x_vals.reshape(head_count, block_count, block_len, head_width).transpose(1, 0, 2, 3)
    dt_blocks = step_dt.reshape(head_count, block_count, block_len).transpose(1, 0, 2)
    dec_blocks = log_decay.reshape(head_count, block_count, block_len).transpose(1, 0, 2)
    b_blocks = b_vals.reshape(block_count, block_len, states)
    c_blocks = c_vals.reshape(block_count, block_len, states)
    doc_blocks = doc_index.reshape(block_count, block_len)
    first_blocks = is_first.reshape(block_count, block_len)
    lower_mask = jnp.arange(block_len)[:, None] >= jnp.arange(block_len)[None, :]

    def advance(carry_state, pieces):
        x_block, dt_block, dec_block, b_block, c_block, doc_block, first_block = pieces
        cumulative = jnp.cumsum(dec_block, axis=1)
        keep_mask = lower_mask & (doc_block[:, None] == doc_block[None, :])
        decay_gaps = jnp.where(
            keep_mask[None], cumulative[:, :, None] - cumulative[:, None, :], 0.0
        )
        scores = jnp.dot(c_block, b_block.T, preferred_element_type=jnp.float32)
        weights = (
            jnp.where(keep_mask[None], jnp.exp(decay_gaps), 0.0)
            * scores[None]
            * dt_block[:, None, :]
        )
        x_float = x_block.astype(jnp.float32)
        inner_part = jnp.einsum("hij,hjp->hip", weights, x_float, precision=highest)
        reach_mask = (jnp.cumsum(first_block) == 0).astype(jnp.float32)
        carried = jnp.einsum(
            "in,hnp->hip", c_block.astype(jnp.float32), carry_state, precision=highest
        )
        carried = carried * (jnp.exp(cumulative) * reach_mask[None])[:, :, None]
        tail_keep = doc_block == doc_block[-1]
        tail_gaps = jnp.where(tail_keep[None], cumulative[:, -1:] - cumulative, 0.0)
        fresh_weight = jnp.where(tail_keep[None], jnp.exp(tail_gaps), 0.0) * dt_block
        written = jnp.einsum(
            "jn,hjp->hnp",
            b_block.astype(jnp.float32),
            x_float * fresh_weight[:, :, None],
            precision=highest,
        )
        kept_share = jnp.exp(cumulative[:, -1]) * reach_mask[-1]
        return (carry_state * kept_share[:, None, None] + written, inner_part + carried)

    initial = jnp.zeros((head_count, states, head_width), jnp.float32)
    final_state, outputs = lax.scan(
        advance,
        initial,
        (x_blocks, dt_blocks, dec_blocks, b_blocks, c_blocks, doc_blocks, first_blocks),
    )
    outputs = outputs.transpose(1, 0, 2, 3).reshape(head_count, length, head_width)
    return (outputs, final_state)


def per_device(
    x_in,
    z_gate,
    b_input,
    c_input,
    dt_raw,
    a_log,
    d_skip,
    norm_gain,
    doc_lengths,
    doc_lang,
    adapt_down,
    adapt_up,
):
    tok_local = x_in.shape[0]
    head_local = dt_raw.shape[0]
    head_width = x_in.shape[1] // head_local
    seq_rank = lax.axis_index("seq")
    head_rank = lax.axis_index("head")
    token_positions = seq_rank * tok_local + jnp.arange(tok_local, dtype=jnp.int32)
    doc_index, is_first, lang_hot = doc_tables(
        doc_lengths, doc_lang, token_positions, adapt_down.shape[0]
    )
    group_index = head_rank * head_local // (SPACE_HEADS // GROUPS)
    b_local = lax.dynamic_index_in_dim(b_input, group_index, axis=1, keepdims=False)
    c_local = lax.dynamic_index_in_dim(c_input, group_index, axis=1, keepdims=False)
    step_dt = jax.nn.softplus(dt_raw)
    log_decay = step_dt * (-jnp.exp(a_log))[:, None]
    x_heads = x_in.reshape(tok_local, head_local, head_width).transpose(1, 0, 2)
    local_out, local_state = block_scan(
        x_heads, step_dt, log_decay, b_local, c_local, doc_index, is_first
    )
    cumulative = jnp.cumsum(log_decay, axis=1)
    reach_mask = (jnp.cumsum(is_first) == 0).astype(jnp.float32)
    through = jnp.exp(cumulative[:, -1]) * reach_mask[-1]

    def combine(earlier, latter):
        return (earlier[0] * latter[0], earlier[1] * latter[0][:, None, None] + latter[1])

    identity = (jnp.ones_like(through), jnp.zeros_like(local_state))
    chain_result = prefix((through, local_state), "seq", combine, identity)
    incoming = chain_result[1]
    entering = jnp.einsum("ln,hnp->hlp", c_local.astype(jnp.float32), incoming, precision=highest)
    entering = entering * (jnp.exp(cumulative) * reach_mask[None])[:, :, None]
    ssd_heads = local_out + entering + d_skip[:, None, None] * x_heads.astype(jnp.float32)
    ssd_rows = ssd_heads.transpose(1, 0, 2).reshape(tok_local, head_local * head_width)
    gated = ssd_rows * jax.nn.silu(z_gate.astype(jnp.float32))
    square_sum = lax.psum(jnp.sum(gated * gated, axis=1), "head")
    mean_square = square_sum / (SPACE_HEADS * HEAD_DIM)
    normed = (gated * lax.rsqrt(mean_square + 1e-05)[:, None] * norm_gain[None, :]).astype(
        jnp.bfloat16
    )
    partial_value = jnp.einsum(
        "td,kdr->tkr", normed, adapt_down, preferred_element_type=jnp.float32
    )
    picked = jnp.sum(jnp.where(lang_hot[:, :, None], partial_value, 0.0), axis=1)
    low_rank = lax.psum(picked, "head").astype(jnp.bfloat16)
    selected = jnp.where(lang_hot[:, :, None], low_rank[:, None, :], jnp.zeros((), jnp.bfloat16))
    selected = selected.reshape(tok_local, adapt_up.shape[0] * adapt_up.shape[1])
    lifted = jnp.dot(
        selected,
        adapt_up.reshape(adapt_up.shape[0] * adapt_up.shape[1], adapt_up.shape[2]),
        preferred_element_type=jnp.float32,
    )
    return (normed.astype(jnp.float32) + lifted).astype(jnp.bfloat16)


def solution(mesh):
    placed = (
        P("seq", "head"),
        P("seq", "head"),
        P("seq", None, None),
        P("seq", None, None),
        P("head", "seq"),
        P("head"),
        P("head"),
        P("head"),
        P(),
        P(),
        P(None, "head", None),
        P(None, None, "head"),
    )
    return jax.shard_map(
        per_device, mesh=mesh, in_specs=placed, out_specs=P("seq", "head"), check_vma=False
    )
```

profile of v0, /device:TPU:64, one launch (start us, length us, event | category | flops | bytes accessed | tf_op | source)
XLA Modules:
  0.0 386.3 jit_solution(6757729792611271632)
XLA Ops:
  9.0 3.3 constant_dynamic-slice_fusion.2
  13.9 64.2 %while.27 = (s32[]{:T(128)}, f32[4,128,128]{1,2,0:T(8,128)S(1)}, f32[8,4,128,128]{3,2,1,0:T(8,128)}, f32[8,4,128]{2,1,0:T(4,128)S(1)}, s32[8,128]{1,0:T(8,128)S(...) while((s32[]{:T(128)}, f32[4,128,128]{1,2,0:T(8,128)S(1)}, ...), condition=%wide.region_6.7_spmd.clone, body=%wide.region_3.0_spmd.clone.sunk | while | flops 307169792 | bytes 2334847 | solution.py:91
  14.5 1.1 compare_bitcast_fusion.2
  20.0 1.8 fusion.94
  22.5 1.1 compare_bitcast_fusion.2
  28.0 1.9 fusion.94
  30.5 1.1 compare_bitcast_fusion.2
  36.0 1.9 fusion.94
  38.5 1.1 compare_bitcast_fusion.2
  44.1 1.9 fusion.94
  46.6 1.1 compare_bitcast_fusion.2
  52.1 1.9 fusion.94
  54.6 1.1 compare_bitcast_fusion.2
  60.1 1.9 fusion.94
  62.6 1.1 compare_bitcast_fusion.2
  68.2 1.9 fusion.94
  70.7 1.1 compare_bitcast_fusion.2
  76.2 1.9 fusion.94
  80.9 1.1 reduce-window.38
  83.2 1.3 dynamic-slice
  85.2 28.6 %all-reduce = f32[64]{0:T(128)S(1)} all-reduce(f32[64]{0:T(128)S(1)} %bitcast_dynamic-update-slice_fusion), channel_id=2, replica_groups=mesh['seq'=16,'head'=32] {'seq'}, use_global_device_ids=true, to_apply=%add | all-reduce | flops 64 | bytes 512
  113.9 2.9 copy.57
  116.8 2.8 reshape.323
  119.7 8.1 %all-gather.4.cloned.1.call-done = f32[64,128,128]{2,1,0:T(8,128)} async-done(((f32[4,128,128]{2,1,0:T(8,128)}), f32[64,128,128]{2,1,0:T(8,128)}) %all-gather.4.cloned.1.call-update) | async-done | bytes 4194320 | tf_op jit(solution)/shard_map/all_gather | solution.py:16
  127.7 17.5 %while.28 = (s32[]{:T(128)}, f32[4,128,128]{2,1,0:T(8,128)S(1)}, s32[]{:T(128)}, f32[16,4]{1,0:T(8,128)S(1)}, f32[16,4,128,128]{3,2,1,0:T(8,128)}, /*index=5*/s32[]{:T(128)}, s32[]{:T(128)}) while((s32[]{:T(128)}, f32[4,128,128]{2,1,0:T(8,128)S(1)}, s32[]{:T(128)}, f32[16,4]{1,0:T(8,128)S(1)}, f32[16,4,128,128]{3,2,1,0:T(8,128)}, ...), condition=%wide.region_12.13_spmd.clone, body=%wide.region_11.12_spmd.clone.sunk | while | flops 262148 | bytes 786593 | solution.py:26
  127.7 1.0 fusion.95
  128.8 1.1 fusion.95
  129.9 1.1 fusion.95
  131.0 1.1 fusion.95
  132.1 1.1 fusion.95
  133.2 1.1 fusion.95
  134.3 1.1 fusion.95
  135.4 1.1 fusion.95
  136.5 1.1 fusion.95
  137.6 1.1 fusion.95
  138.7 1.1 fusion.95
  139.8 1.1 fusion.95
  140.9 1.1 fusion.95
  142.0 1.1 fusion.95
  143.1 1.1 fusion.95
  144.2 1.1 fusion.95
  145.3 4.2 %fusion.52 = f32[4,1024,128]{1,2,0:T(8,128)} fusion(f32[4,1024,128]{1,2,0:T(8,128)} %reshape.323, bf16[4,1024,128]{1,2,0:T(8,128)(2,1)S(1)} %bitcast.150, f32[4,128,128]{2,1,0:T(8,128)S(1)} %get-tuple-element.159, f32[4]{0:T(128)S(1)} %copy-done.8, f32[4,1024]{1,0:T(4,128)S(1)} %exponential_multiply_fusion.2, bf16[1024,1,128]{2,0,1:T(8,128)(2,1)S(1)} %bitcast.153), kind=kOutput, calls=%fused_computation.71 | convolution fusion | flops 807927808 | bytes 5783568 | tf_op jit(solution)/shard_map/ln,hnp->hlp/dot_general | solution.py:142
  149.5 3.0 copy.62
  152.6 3.6 multiply_reduce_fusion
  156.2 74.6 %psum.14 = f32[1024]{0:T(1024)S(1)} all-reduce(f32[1024]{0:T(1024)S(1)} %get-tuple-element.247), channel_id=1, replica_groups=mesh['seq'=16,'head'=32] {'head'}, use_global_device_ids=true, to_apply=%region_14.15 | all-reduce | flops 1024 | bytes 8192 | tf_op jit(solution)/shard_map/psum | solution.py:147
  230.8 2.4 select_reduce_fusion
  233.3 142.1 %all-reduce.2 = bf16[1024,128]{1,0:T(8,128)(2,1)S(1)} all-reduce(f32[1024,128]{1,0:T(8,128)S(1)} %select_reduce_fusion), channel_id=1, replica_groups=mesh['seq'=16,'head'=32] {'head'}, use_global_device_ids=true, to_apply=%region_17.18 | all-reduce | flops 131072 | bytes 786432 | tf_op jit(solution)/shard_map/psum | solution.py:156
  375.4 4.0 %fusion.51 = bf16[1024,512]{1,0:T(8,128)(2,1)} fusion(bf16[4,128,512]{2,1,0:T(8,128)(2,1)S(1)} %copy-done, pred[1024,4]{0,1:T(4,128)(4,1)S(1)} %iota_compare_fusion.2, bf16[1024,128]{1,0:T(8,128)(2,1)S(1)} %all-reduce.2, f32[512]{0:T(512)S(1)} %copy-done.11, f32[1024,512]{1,0:T(8,128)} %get-tuple-element.248, f32[1024]{0:T(1024)S(1)} %add_rsqrt_fusion), kind=kOutput, calls=%fused_computation.69 | convolution fusion | flops 540540928 | bytes 3942400 | tf_op jit(solution)/shard_map/dot_general | solution.py:159
  (261 shorter events, 48.0 us)
Async XLA Ops:
  6.5 368.9 %copy-start = (bf16[4,128,512]{2,1,0:T(8,128)(2,1)S(1)}, bf16[4,128,512]{2,1,0:T(8,128)(2,1)}, u32[]{:S(2)}) copy-start(bf16[4,128,512]{2,1,0:T(8,128)(2,1)} %param.27) | copy-start | bytes 1572868
  6.5 5.8 %copy-start.1 = (bf16[1024,512]{1,0:T(8,128)(2,1)S(1)}, bf16[1024,512]{1,0:T(8,128)(2,1)}, u32[]{:S(2)}) copy-start(bf16[1024,512]{1,0:T(8,128)(2,1)} %param.16) | copy-start | bytes 3145732
  6.5 121.2 %all-gather.4.cloned.1.call-start = ((), (), s32[]{:S(2)}) async-start(), calls=%async_computation | async-start | bytes 4456448 | tf_op jit(solution)/shard_map/all_gather | solution.py:16
  12.4 0.8 copy-start.5
  13.9 1.7 copy-start.6
  13.9 2.9 copy-start.3
  17.2 4.7 %copy-start.4 = (f32[8,4,128]{2,1,0:T(4,128)S(1)}, f32[8,4,128]{2,1,0:T(4,128)}, u32[]{:S(2)}) copy-start(f32[8,4,128]{2,1,0:T(4,128)} %copy-done.3) | copy-start | bytes 49156 | tf_op jit(solution)/shard_map/while
  17.2 4.7 %copy-start.7 = (s32[8,128]{1,0:T(8,128)S(1)}, s32[8,128]{1,0:T(8,128)}, u32[]{:S(2)}) copy-start(s32[8,128]{1,0:T(8,128)} %copy-done.6) | copy-start | bytes 12292 | tf_op jit(solution)/shard_map/while
  21.9 1.7 copy-start.6
  21.9 2.9 copy-start.3
  25.2 4.7 %copy-start.4 = (f32[8,4,128]{2,1,0:T(4,128)S(1)}, f32[8,4,128]{2,1,0:T(4,128)}, u32[]{:S(2)}) copy-start(f32[8,4,128]{2,1,0:T(4,128)} %copy-done.3) | copy-start | bytes 49156 | tf_op jit(solution)/shard_map/while
  25.2 4.7 %copy-start.7 = (s32[8,128]{1,0:T(8,128)S(1)}, s32[8,128]{1,0:T(8,128)}, u32[]{:S(2)}) copy-start(s32[8,128]{1,0:T(8,128)} %copy-done.6) | copy-start | bytes 12292 | tf_op jit(solution)/shard_map/while
  29.9 1.7 copy-start.6
  29.9 2.9 copy-start.3
  33.2 4.7 %copy-start.4 = (f32[8,4,128]{2,1,0:T(4,128)S(1)}, f32[8,4,128]{2,1,0:T(4,128)}, u32[]{:S(2)}) copy-start(f32[8,4,128]{2,1,0:T(4,128)} %copy-done.3) | copy-start | bytes 49156 | tf_op jit(solution)/shard_map/while
  33.2 4.7 %copy-start.7 = (s32[8,128]{1,0:T(8,128)S(1)}, s32[8,128]{1,0:T(8,128)}, u32[]{:S(2)}) copy-start(s32[8,128]{1,0:T(8,128)} %copy-done.6) | copy-start | bytes 12292 | tf_op jit(solution)/shard_map/while
  37.9 1.7 copy-start.6
  37.9 2.9 copy-start.3
  41.3 4.7 %copy-start.4 = (f32[8,4,128]{2,1,0:T(4,128)S(1)}, f32[8,4,128]{2,1,0:T(4,128)}, u32[]{:S(2)}) copy-start(f32[8,4,128]{2,1,0:T(4,128)} %copy-done.3) | copy-start | bytes 49156 | tf_op jit(solution)/shard_map/while
  41.3 4.7 %copy-start.7 = (s32[8,128]{1,0:T(8,128)S(1)}, s32[8,128]{1,0:T(8,128)}, u32[]{:S(2)}) copy-start(s32[8,128]{1,0:T(8,128)} %copy-done.6) | copy-start | bytes 12292 | tf_op jit(solution)/shard_map/while
  46.0 1.7 copy-start.6
  46.0 2.9 copy-start.3
  49.3 4.7 %copy-start.4 = (f32[8,4,128]{2,1,0:T(4,128)S(1)}, f32[8,4,128]{2,1,0:T(4,128)}, u32[]{:S(2)}) copy-start(f32[8,4,128]{2,1,0:T(4,128)} %copy-done.3) | copy-start | bytes 49156 | tf_op jit(solution)/shard_map/while
  49.3 4.7 %copy-start.7 = (s32[8,128]{1,0:T(8,128)S(1)}, s32[8,128]{1,0:T(8,128)}, u32[]{:S(2)}) copy-start(s32[8,128]{1,0:T(8,128)} %copy-done.6) | copy-start | bytes 12292 | tf_op jit(solution)/shard_map/while
  54.0 1.7 copy-start.6
  54.0 2.9 copy-start.3
  57.3 4.7 %copy-start.4 = (f32[8,4,128]{2,1,0:T(4,128)S(1)}, f32[8,4,128]{2,1,0:T(4,128)}, u32[]{:S(2)}) copy-start(f32[8,4,128]{2,1,0:T(4,128)} %copy-done.3) | copy-start | bytes 49156 | tf_op jit(solution)/shard_map/while
  57.3 4.7 %copy-start.7 = (s32[8,128]{1,0:T(8,128)S(1)}, s32[8,128]{1,0:T(8,128)}, u32[]{:S(2)}) copy-start(s32[8,128]{1,0:T(8,128)} %copy-done.6) | copy-start | bytes 12292 | tf_op jit(solution)/shard_map/while
  62.0 1.7 copy-start.6
  62.0 2.9 copy-start.3
  65.4 4.7 %copy-start.4 = (f32[8,4,128]{2,1,0:T(4,128)S(1)}, f32[8,4,128]{2,1,0:T(4,128)}, u32[]{:S(2)}) copy-start(f32[8,4,128]{2,1,0:T(4,128)} %copy-done.3) | copy-start | bytes 49156 | tf_op jit(solution)/shard_map/while
  65.4 4.7 %copy-start.7 = (s32[8,128]{1,0:T(8,128)S(1)}, s32[8,128]{1,0:T(8,128)}, u32[]{:S(2)}) copy-start(s32[8,128]{1,0:T(8,128)} %copy-done.6) | copy-start | bytes 12292 | tf_op jit(solution)/shard_map/while
  70.1 1.7 copy-start.6
  70.1 2.9 copy-start.3
  73.4 4.7 %copy-start.4 = (f32[8,4,128]{2,1,0:T(4,128)S(1)}, f32[8,4,128]{2,1,0:T(4,128)}, u32[]{:S(2)}) copy-start(f32[8,4,128]{2,1,0:T(4,128)} %copy-done.3) | copy-start | bytes 49156 | tf_op jit(solution)/shard_map/while
  73.4 4.7 %copy-start.7 = (s32[8,128]{1,0:T(8,128)S(1)}, s32[8,128]{1,0:T(8,128)}, u32[]{:S(2)}) copy-start(s32[8,128]{1,0:T(8,128)} %copy-done.6) | copy-start | bytes 12292 | tf_op jit(solution)/shard_map/while
  116.8 2.8 copy-start.9
  119.6 25.7 %copy-start.8 = (f32[4]{0:T(128)S(1)}, f32[4]{0:T(128)}, u32[]{:S(2)}) copy-start(f32[4]{0:T(128)} %param.22) | copy-start | bytes 52
  149.5 3.0 copy-start.2
  152.6 78.3 %copy-start.10 = (bf16[4,512,128]{2,1,0:T(8,128)(2,1)S(1)}, bf16[4,512,128]{2,1,0:T(8,128)(2,1)}, u32[]{:S(2)}) copy-start(bf16[4,512,128]{2,1,0:T(8,128)(2,1)} %param.26) | copy-start | bytes 1572868
  152.6 78.3 %copy-start.11 = (f32[512]{0:T(512)S(1)}, f32[512]{0:T(512)}, u32[]{:S(2)}) copy-start(f32[512]{0:T(512)} %param.23) | copy-start | bytes 6148
Sparse Core Ops, SparseCore 0:
  79.1 48.6 all-gather.3
where the time goes:
time: 388 us; the launch traced here: 386 us
  blocking collectives  245 us (63%)
  other arithmetic  56.7 us (15%)
  matrix products  32.3 us (8%)
  local copies, waits for them, and re-layouts  28.7 us (7%)
  between operations  14.2 us (4%)
  waiting for transfers between devices  8.07 us (2%)
    psum x1, blocking collectives, per_device(): low_rank = lax.psum(picked, 'head').astype(jnp.bfloat16)  142 us
    psum x1, blocking collectives, per_device(): square_sum = lax.psum(jnp.sum(gated * gated, axis=1), 'head')  74.6 us
    unnamed x1, blocking collectives  28.6 us
    select_n x16, other arithmetic, hop(): return jax.tree.map(lambda a, b: jnp.where(reached, a, b), new, before)  16.9 us
    dot_general x8, matrix products, advance(): inner_part = jnp.einsum('hij,hjp->hip', weights, x_float, precision=highest)  15 us
    broadcast_in_dim x8, other arithmetic, advance(): jnp.where(tail_keep[None], jnp.exp(tail_gaps), 0.0) * dt_block  9.09 us
    all_gather x1, waiting for transfers between devices, prefix(): everything = jax.tree.map(lambda part: lax.all_gather(part, axis), x)  8.05 us
  transfers between devices with their start and end apart: 1, of which 1 were waited for; matrix products, arithmetic and copies ran while one was open for 3% of the time, Pallas kernels for 0%

commit v1 on v0

v1 whole, which is shorter than its diff:
```python
import functools

import jax
import jax.numpy as jnp
from jax import lax
from jax.experimental import pallas as pl
from jax.experimental.pallas import tpu as pltpu
from jax.sharding import PartitionSpec as P

SPACE_HEADS = 128
HEAD_DIM = 128
GROUPS = 8
L = 128
MESH = pl.DeviceIdType.MESH
F32 = jnp.float32
BF16 = jnp.bfloat16
HIGHEST = lax.Precision.HIGHEST


def nt(a, b, precision=None):
    return lax.dot_general(
        a, b, (((1,), (1,)), ((), ())), preferred_element_type=F32, precision=precision
    )


def mm(a, b, precision=None):
    return jnp.dot(a, b, preferred_element_type=F32, precision=precision)


def kernel_body(
    seq_n,
    xn,
    yn,
    doc_len,
    doc_lang,
    a_log,
    d_skip,
    dt_ref,
    gain_ref,
    x_hbm,
    z_hbm,
    b_hbm,
    c_hbm,
    down_hbm,
    up_hbm,
    out_hbm,
    x_s,
    z_s,
    b_s,
    c_s,
    a_s,
    u_s,
    ypre,
    sz,
    g_s,
    out_s,
    dt32,
    rowb,
    rows,
    wdev,
    colb,
    csel,
    bsel,
    bt,
    state,
    s_mine,
    s_part,
    d_mine,
    d_part,
    c_send,
    q1,
    dc_send,
    dq1,
    t_send,
    q2,
    h_mine,
    h_part,
    hb,
    pbuf,
    rx,
    qsum,
    ry,
    lbuf,
    ss_mine,
    ss_rx,
    ss_x,
    ss_ry,
    colscale,
    in_sem,
    out_sem,
    sa_sem,
    ra_sem,
    sx_sem,
    rx_sem,
    sy_sem,
    ry_sem,
    sgy_sem,
    rgy_sem,
    sgx_sem,
    rgx_sem,
    ssx_s,
    ssx_r,
    ssy_s,
    ssy_r,
):
    tok = x_s.shape[0]
    nc = tok // L
    nh = dt_ref.shape[0]
    qt = tok // xn
    pt = qt // yn
    rank = lax.axis_index("seq")
    hd = lax.axis_index("head")
    core = lax.rem(rank, 2)
    z = rank // 2
    nz = seq_n // 2
    mx = hd // yn
    my = lax.rem(hd, yn)
    group = hd * nh // (SPACE_HEADS // GROUPS)

    def seq_dev(dz):
        return (lax.rem(z + dz + nz, nz) * 2 + core, hd)

    partner = (z * 2 + 1 - core, hd)

    def x_dev(i):
        return (rank, lax.rem(mx + i, xn) * yn + my)

    def y_dev(i):
        return (rank, mx * yn + lax.rem(my + i, yn))

    chain = nz > 4
    peers = [partner]
    if chain:
        peers += [seq_dev(d) for d in (1, -1, 2, -2)]
    peers += [x_dev(i) for i in range(1, xn)]
    peers += [y_dev(i) for i in range(1, yn)]
    barrier = pltpu.get_barrier_semaphore()
    for peer in peers:
        pl.semaphore_signal(barrier, inc=1, device_id=peer, device_id_type=MESH)

    def load(src, dst, k):
        copy = pltpu.make_async_copy(src, dst, in_sem.at[k])
        copy.start()
        return copy

    b_in = load(b_hbm, b_s, 0)
    x_in = load(x_hbm, x_s, 1)
    c_in = load(c_hbm, c_s, 2)
    z_in = load(z_hbm, z_s, 3)
    a_in = [load(down_hbm.at[k], a_s.at[:, pl.ds(k * 128, 128)], 4 + k) for k in range(4)]
    u_in = load(up_hbm, u_s, 8)

    for c in range(nc):
        dt32[pl.ds(c * nh, nh), :] = dt_ref[:, pl.ds(c * L, L)]
    shape = (nc * nh, L)
    rid = lax.broadcasted_iota(jnp.int32, shape, 0)
    lane = lax.broadcasted_iota(jnp.int32, shape, 1)
    head_of = rid % nh
    chunk_of = rid // nh
    raw = dt32[...]
    dt = jnp.maximum(raw, 0.0) + jnp.log1p(jnp.exp(-jnp.abs(raw)))
    alog = jnp.full(shape, a_log[0], F32)
    for h in range(1, nh):
        alog = jnp.where(head_of == h, a_log[h], alog)
    ld = dt * -jnp.exp(alog)
    ki = lax.broadcasted_iota(jnp.int32, (L, L), 0)
    kj = lax.broadcasted_iota(jnp.int32, (L, L), 1)
    cum = mm(ld, (ki <= kj).astype(F32), HIGHEST)
    suf = mm(ld, (ki > kj).astype(F32), HIGHEST)
    tot = jnp.broadcast_to(jnp.sum(ld, axis=1, keepdims=True), shape)

    def down(v, k):
        return jnp.where(rid >= k, pltpu.roll(v, k, 0), 0.0)

    def up(v, k):
        return jnp.where(rid < nc * nh - k, pltpu.roll(v, nc * nh - k, 0), 0.0)

    pre, post = (down(tot, nh), up(tot, nh))
    step = nh
    while step < nc * nh:
        pre = pre + down(pre, step)
        post = post + up(post, step)
        step *= 2
    starts, first = ([], jnp.int32(0))
    for k in range(doc_len.shape[0]):
        starts.append(first)
        first = first + doc_len[k]
    base = rank * tok

    def docs(t):
        total = None
        for s in starts:
            one = (t >= s).astype(jnp.int32)
            total = one if total is None else total + one
        return total

    n_t = docs(base + chunk_of * L + lane)
    n_cs = docs(base + chunk_of * L - 1)
    n_ce = docs(base + chunk_of * L + (L - 1))
    n_bs = docs(base + 0 * chunk_of - 1)
    n_be = docs(base + 0 * chunk_of + (tok - 1))
    lang = jnp.zeros(shape, jnp.int32)
    for k in range(doc_lang.shape[0]):
        lang = jnp.where(n_t == k + 1, doc_lang[k], lang)

    def keep(cond, v):
        return jnp.where(cond, v, 0.0)

    carry = keep(n_t == n_cs, jnp.exp(cum))
    enter = keep(n_t == n_bs, jnp.exp(pre + cum))
    w_dev = keep(n_t == n_be, jnp.exp(suf + post)) * dt
    w_chunk = keep(n_t == n_ce, jnp.exp(suf)) * dt
    kept = keep(n_ce == n_cs, jnp.exp(tot))
    through = keep(n_be == n_bs, jnp.exp(pre + tot))
    n_f = n_t.astype(F32)
    lang_f = lang.astype(F32)
    for c in range(nc):
        own = slice(c * nh, (c + 1) * nh)
        for k, v in enumerate((cum, carry, enter)):
            rowb[c, k * nh : (k + 1) * nh, :] = v[own]
        rowb[c, 12:13, :] = n_f[c * nh : c * nh + 1]
        rowb[c, 13:14, :] = lang_f[c * nh : c * nh + 1]
        rowb[c, 14:16, :] = jnp.zeros((2, L), F32)
        for k, v in enumerate((cum, dt, w_chunk, kept)):
            rows[c, k * nh : (k + 1) * nh, :] = v[own]
        rows[c, 16:17, :] = n_f[c * nh : c * nh + 1]
        wdev[:, c * L : (c + 1) * L] = w_dev[own]
    for h in range(nh):
        r = (nc - 1) * nh + h
        d_mine[h // 2, :, (h % 2) * 128 : (h % 2 + 1) * 128] = jnp.broadcast_to(
            through[r : r + 1], (8, L)
        )
    cols = jnp.transpose(rowb[...].reshape(nc * 16, L))
    for c in range(nc):
        colb[c, :, 0:16] = cols[:, c * 16 : (c + 1) * 16]

    pr = lax.broadcasted_iota(jnp.int32, (L, L * GROUPS), 0)
    pc = lax.broadcasted_iota(jnp.int32, (L, L * GROUPS), 1)
    pick = (pc == pr * GROUPS + group).astype(BF16)
    b_in.wait()
    for c in range(nc):
        part = mm(pick, b_s[c * L * GROUPS : (c + 1) * L * GROUPS, :])
        bsel[c] = part.astype(BF16)
        bt[:, c * L : (c + 1) * L] = jnp.transpose(part)
    x_in.wait()
    for h in range(nh):
        lhs = (bt[...] * wdev[h : h + 1, :]).astype(BF16)
        s_mine[h // 2, :, (h % 2) * 128 : (h % 2 + 1) * 128] = mm(
            lhs, x_s[:, h * 128 : (h + 1) * 128]
        )
    pl.semaphore_wait(barrier, len(peers))

    def send(src, dst, s_sem, r_sem, dev):
        copy = pltpu.make_async_remote_copy(
            src_ref=src, dst_ref=dst, send_sem=s_sem, recv_sem=r_sem,
            device_id=dev, device_id_type=MESH,
        )
        copy.start()
        return copy

    other = 1 - core
    pair = [
        send(s_mine.at[other], s_part.at[other], sa_sem.at[0], ra_sem.at[0], partner),
        send(d_mine, d_part, sa_sem.at[1], ra_sem.at[1], partner),
        send(s_mine.at[core], s_part.at[core], sa_sem.at[2], ra_sem.at[2], partner),
    ]

    c_in.wait()
    for c in range(nc):
        csel[c] = mm(pick, c_s[c * L * GROUPS : (c + 1) * L * GROUPS, :]).astype(BF16)

    pair[0].wait_recv()
    pair[1].wait_recv()
    is_second = core == 1
    if chain:
        sm, sp = s_mine[core], s_part[core]
        dm, dp = d_mine[core][0:1], d_part[core][0:1]
        earlier = jnp.where(is_second, sp, sm)
        latter = jnp.where(is_second, sm, sp)
        d_latter = jnp.where(is_second, dm, dp)
        chip_s = d_latter * earlier + latter
        chip_d = dm * dp
        h_mine[...] = chip_s
        c_send[...] = chip_s.astype(BF16)
        dc_send[...] = jnp.broadcast_to(chip_d, dc_send.shape)
        ring = [
            send(c_send, q1, sa_sem.at[3], ra_sem.at[3], seq_dev(1)),
            send(dc_send, dq1, sa_sem.at[4], ra_sem.at[4], seq_dev(1)),
        ]

    state[...] = jnp.zeros_like(state)
    lower = ki >= kj

    def chunk(c, carry_in):
        at = pl.multiple_of(c * L, L)
        col = colb[c]
        row = rows[c]
        cc = csel[c]
        gram = nt(cc, bsel[c])
        same = col[:, 12:13] == row[16:17]
        gram = jnp.where(same & lower, gram, 0.0)
        cf = cc.astype(F32)
        btc = bt[:, pl.ds(at, L)]
        for h in range(nh):
            hs = slice(h * 128, (h + 1) * 128)
            gap = jnp.minimum(col[:, h : h + 1] - row[h : h + 1], 0.0)
            w = (gram * jnp.exp(gap) * row[nh + h : nh + h + 1]).astype(BF16)
            xh = x_s[pl.ds(at, L), hs]
            st = state[h]
            cw = (cf * col[:, nh + h : nh + h + 1]).astype(BF16)
            y = mm(w, xh) + mm(cw, st.astype(BF16)) + d_skip[h] * xh.astype(F32)
            ypre[pl.ds(at, L), hs] = y
            new = (btc * row[2 * nh + h : 2 * nh + h + 1]).astype(BF16)
            state[h] = st * row[3 * nh + h : 3 * nh + h + 1] + mm(new, xh)
        return carry_in

    def silu(c, carry_in):
        at = pl.multiple_of(c * L, L)
        for h in range(nh):
            hs = slice(h * 128, (h + 1) * 128)
            v = z_s[pl.ds(at, L), hs].astype(F32)
            sz[pl.ds(at, L), hs] = v / (1.0 + jnp.exp(-v))
        return carry_in

    cut = nc // 2
    lax.fori_loop(0, cut, chunk, 0)

    if chain:
        ring[0].wait_recv()
        ring[1].wait_recv()
        from1 = jnp.where(z >= 1, q1[...].astype(F32), 0.0)
        t_send[...] = (h_mine[...] + chip_d * from1).astype(BF16)
        far = send(t_send, q2, sa_sem.at[5], ra_sem.at[5], seq_dev(2))
    z_in.wait()
    lax.fori_loop(cut, nc, chunk, 0)
    lax.fori_loop(0, nc // 2, silu, 0)
    pair[2].wait_recv()
    for copy in pair:
        copy.wait_send()
    if chain:
        far.wait_recv()
        from1 = jnp.where(z >= 1, q1[...].astype(F32), 0.0)
        from2 = jnp.where(z >= 2, q2[...].astype(F32), 0.0)
        h_mine[...] = from1 + dq1[0:1, :] * from2
        back = send(h_mine, h_part, sa_sem.at[6], ra_sem.at[6], partner)
        lax.fori_loop(nc // 2, nc, silu, 0)
        back.wait_recv()
        for half in range(2):
            inc = jnp.where(core == half, h_mine[...], h_part[...])
            second = d_part[half][0:1] * inc + s_part[half]
            hb[half] = jnp.where(is_second, second, inc).astype(BF16)
        back.wait_send()
        far.wait_send()
        for copy in ring:
            copy.wait_send()
    else:
        lax.fori_loop(nc // 2, nc, silu, 0)
        for half in range(2):
            hb[half] = jnp.where(is_second, s_part[half], 0.0).astype(BF16)

    for copy in a_in:
        copy.wait()
    per_q = qt // L
    one8 = jnp.ones((8, L), F32)

    def gate(q):
        def body(i, carry_in):
            c = q * per_q + i
            at = pl.multiple_of(c * L, L)
            col = colb[c]
            cc = csel[c]
            sq = None
            for h in range(nh):
                hs = slice(h * 128, (h + 1) * 128)
                hw = hb[h // 2, :, (h % 2) * 128 : (h % 2 + 1) * 128]
                ent = mm(cc, hw) * col[:, 2 * nh + h : 2 * nh + h + 1]
                gated = (ypre[pl.ds(at, L), hs] + ent) * sz[pl.ds(at, L), hs]
                sq = gated * gated if sq is None else sq + gated * gated
                g_s[pl.ds(at, L), hs] = (gated * gain_ref[0:1, hs]).astype(BF16)
            ss_mine[pl.ds(c, 1), :] = nt(one8, sq, HIGHEST)[0:1]
            g = g_s[pl.ds(at, L), :]
            lg = col[:, 13:14]
            picked = None
            for k in range(0, 4, 2):
                two = mm(g, a_s[:, k * 128 : (k + 2) * 128])
                for j in range(2):
                    one = jnp.where(lg == float(k + j), two[:, j * 128 : (j + 1) * 128], 0.0)
                    picked = one if picked is None else picked + one
            pbuf[q, pl.ds(pl.multiple_of(i * L, L), L), :] = picked.astype(BF16)
            return carry_in

        lax.fori_loop(0, per_q, body, 0)

    sends = []
    order = sorted(range(1, xn), key=lambda i: -min(i, xn - i))
    for i in order:
        q = lax.rem(mx + i, xn)
        gate(q)
        sends.append(send(pbuf.at[q], rx.at[mx], sx_sem.at[i], rx_sem.at[mx], x_dev(i)))
    gate(mx)
    for i in order:
        sends.append(send(ss_mine, ss_rx.at[mx], ssx_s.at[i], ssx_r.at[mx], x_dev(i)))

    def arrived(dst, sem):
        pltpu.make_async_remote_copy(
            src_ref=dst, dst_ref=dst, send_sem=in_sem.at[0], recv_sem=sem,
            device_id=partner, device_id_type=MESH,
        ).wait_recv()

    total = pbuf[mx].astype(F32)
    for i in order[::-1]:
        src = lax.rem(mx + i, xn)
        arrived(rx.at[src], rx_sem.at[src])
        total = total + rx[src].astype(F32)
    qsum[...] = total.astype(BF16).reshape(qsum.shape)
    y_order = sorted(range(1, yn), key=lambda i: -min(i, yn - i))
    for i in y_order:
        p = lax.rem(my + i, yn)
        sends.append(send(qsum.at[p], ry.at[my], sy_sem.at[i], ry_sem.at[my], y_dev(i)))
    ss = ss_mine[...]
    for i in order[::-1]:
        src = lax.rem(mx + i, xn)
        arrived(ss_rx.at[src], ssx_r.at[src])
        ss = ss + ss_rx[src]
    ss_x[...] = ss
    for i in y_order:
        sends.append(send(ss_x, ss_ry.at[my], ssy_s.at[i], ssy_r.at[my], y_dev(i)))
    piece = qsum[my].astype(F32)
    for i in y_order[::-1]:
        src = lax.rem(my + i, yn)
        arrived(ry.at[src], ry_sem.at[src])
        piece = piece + ry[src].astype(F32)
    lbuf[mx, my] = piece.astype(BF16)
    for i in y_order:
        sends.append(send(lbuf.at[mx, my], lbuf.at[mx, my], sgy_sem.at[i], rgy_sem.at[my], y_dev(i)))

    def forward(p, k):
        for i in order:
            sends.append(
                send(lbuf.at[mx, p], lbuf.at[mx, p], sgx_sem.at[i, k], rgx_sem.at[mx], x_dev(i))
            )

    forward(my, 0)

    for i in y_order[::-1]:
        src = lax.rem(my + i, yn)
        arrived(ss_ry.at[src], ssy_r.at[src])
        ss = ss + ss_ry[src]
    scale = lax.rsqrt(ss / (SPACE_HEADS * HEAD_DIM) + 1e-05)
    eye = ki == kj
    for c in range(nc):
        spread = jnp.broadcast_to(scale[c : c + 1], (L, L))
        one = jnp.sum(jnp.where(eye, spread, 0.0), axis=1, keepdims=True)
        colscale[c] = jnp.broadcast_to(one, (L, L))

    for i in y_order[::-1]:
        p = lax.rem(my + i, yn)
        arrived(lbuf.at[mx, p], rgy_sem.at[p])
        forward(p, i)

    u_in.wait()

    def finish(q):
        def body(i, carry_in):
            c = q * per_q + i
            at = pl.multiple_of(c * L, L)
            lg = colb[c][:, 13:14]
            if pt > L:
                low = lbuf[q, 0, pl.ds(pl.multiple_of(i * L, L), L)].astype(F32)
            else:
                per = L // pt
                low = lbuf[q, pl.ds(i * per, per)].reshape(L, 128).astype(F32)
            sel = jnp.concatenate(
                [jnp.where(lg == float(k), low, 0.0).astype(BF16) for k in range(4)], axis=1
            )
            scl = colscale[c]
            for h in range(0, nh, 2):
                lift = mm(sel, u_s[:, h * 128 : (h + 2) * 128])
                for j in range(2):
                    hs = slice((h + j) * 128, (h + j + 1) * 128)
                    val = g_s[pl.ds(at, L), hs].astype(F32) + lift[:, j * 128 : (j + 1) * 128]
                    out_s[pl.ds(at, L), hs] = (val * scl).astype(BF16)
            return carry_in

        lax.fori_loop(0, per_q, body, 0)
        at = pl.multiple_of(q * qt, qt)
        copy = pltpu.make_async_copy(
            out_s.at[pl.ds(at, qt), :], out_hbm.at[pl.ds(at, qt), :], out_sem.at[q]
        )
        copy.start()
        return copy

    outs = [finish(mx)]
    for i in order[::-1]:
        q = lax.rem(mx + i, xn)
        arrived(lbuf.at[q], rgx_sem.at[q])
        outs.append(finish(q))
    for copy in sends:
        copy.wait_send()
    for copy in outs:
        copy.wait()


def per_device(seq_n, xn, yn, x_in, z_gate, b_input, c_input, dt_raw, a_log, d_skip, norm_gain,
               doc_lengths, doc_lang, adapt_down, adapt_up):
    tok, feat = x_in.shape
    nh = dt_raw.shape[0]
    nc = tok // L
    qt = tok // xn
    pt = qt // yn
    half = feat // 2
    dma = pltpu.SemaphoreType.DMA
    vm = pltpu.VMEM
    scratch = [
        vm((tok, feat), BF16),
        vm((tok, feat), BF16),
        vm((tok * GROUPS, 128), BF16),
        vm((tok * GROUPS, 128), BF16),
        vm((feat, 512), BF16),
        vm((512, feat), BF16),
        vm((tok, feat), F32),
        vm((tok, feat), F32),
        vm((tok, feat), BF16),
        vm((tok, feat), BF16),
        vm((nc * nh, L), F32),
        vm((nc, 16, L), F32),
        vm((nc, 24, L), F32),
        vm((nh, tok), F32),
        vm((nc, L, L), F32),
        vm((nc, L, L), BF16),
        vm((nc, L, L), BF16),
        vm((L, tok), F32),
        vm((nh, 128, 128), F32),
        vm((2, 128, half), F32),
        vm((2, 128, half), F32),
        vm((2, 8, half), F32),
        vm((2, 8, half), F32),
        vm((128, half), BF16),
        vm((128, half), BF16),
        vm((8, half), F32),
        vm((8, half), F32),
        vm((128, half), BF16),
        vm((128, half), BF16),
        vm((128, half), F32),
        vm((128, half), F32),
        vm((2, 128, half), BF16),
        vm((xn, qt, 128), BF16),
        vm((xn, qt, 128), BF16),
        vm((yn, pt, 128), BF16),
        vm((yn, pt, 128), BF16),
        vm((xn, yn, pt, 128), BF16),
        vm((nc, L), F32),
        vm((xn, nc, L), F32),
        vm((nc, L), F32),
        vm((yn, nc, L), F32),
        vm((nc, L, L), F32),
        dma((9,)),
        dma((xn,)),
        dma((7,)),
        dma((7,)),
        dma((xn,)),
        dma((xn,)),
        dma((yn,)),
        dma((yn,)),
        dma((yn,)),
        dma((yn,)),
        dma((xn, yn)),
        dma((xn,)),
        dma((xn,)),
        dma((xn,)),
        dma((yn,)),
        dma((yn,)),
    ]
    smem = pl.BlockSpec(memory_space=pltpu.SMEM)
    vmem = pl.BlockSpec(memory_space=pltpu.VMEM)
    hbm = pl.BlockSpec(memory_space=pl.ANY)
    return pl.pallas_call(
        functools.partial(kernel_body, seq_n, xn, yn),
        out_shape=jax.ShapeDtypeStruct((tok, feat), BF16),
        in_specs=[smem] * 4 + [vmem] * 2 + [hbm] * 6,
        out_specs=hbm,
        scratch_shapes=scratch,
        compiler_params=pltpu.CompilerParams(
            collective_id=0, has_side_effects=True, vmem_limit_bytes=48 * 1024 * 1024
        ),
    )(
        doc_lengths,
        doc_lang,
        a_log,
        d_skip,
        dt_raw,
        norm_gain.reshape(1, feat),
        x_in,
        z_gate,
        b_input.reshape(tok * GROUPS, 128),
        c_input.reshape(tok * GROUPS, 128),
        adapt_down,
        adapt_up.reshape(512, feat),
    )


def solution(mesh):
    seq_n, head_n = mesh.shape["seq"], mesh.shape["head"]
    xn = 4 if head_n == 32 else min(2, head_n)
    placed = (
        P("seq", "head"),
        P("seq", "head"),
        P("seq", None, None),
        P("seq", None, None),
        P("head", "seq"),
        P("head"),
        P("head"),
        P("head"),
        P(),
        P(),
        P(None, "head", None),
        P(None, None, "head"),
    )
    return jax.shard_map(
        functools.partial(per_device, seq_n, xn, head_n // xn),
        mesh=mesh, in_specs=placed, out_specs=P("seq", "head"), check_vma=False,
    )
```

time: 388 us -> 57.7 us (0.15)
  blocking collectives: 245 us -> 0 us
  other arithmetic: 56.7 us -> 0 us
  Pallas kernels: 0 us -> 47.8 us
  matrix products: 32.3 us -> 0 us
  local copies, waits for them, and re-layouts: 28.7 us -> 9.52 us
  between operations: 14.2 us -> 0.02 us
  waiting for transfers between devices: 8.07 us -> 0 us
    psum x2 -> x0, blocking collectives: 217 us -> none  [the longest x1 142 us: per_device(): low_rank = lax.psum(picked, 'head').astype(jnp.bfloat16)]
    pallas_call x0 -> x1, Pallas kernels: none -> 47.8 us  [per_device(): pl.pallas_call(functools.partial(kernel_body, seq_n, xn, yn), out_shape=j...]
    dot_general x35 -> x0, matrix products: 32.3 us -> none  [the longest x8 15 us: advance(): inner_part = jnp.einsum('hij,hjp->hip', weights, x_float, precision=highest)]
    unnamed x1 -> x0, blocking collectives: 28.6 us -> none
    select_n x16 -> x0, other arithmetic: 16.9 us -> none  [hop(): return jax.tree.map(lambda a, b: jnp.where(reached, a, b), new, before)]
    mul x18 -> x0, other arithmetic: 11.9 us -> none  [the longest x8 6.12 us: advance(): jnp.where(tail_keep[None], jnp.exp(tail_gaps), 0.0) * dt_block]
    slice x26 -> x0, local copies, waits for them, and re-layouts: 11.2 us -> none  [the longest x16 5.81 us: advance(): kept_share = jnp.exp(cumulative[:, -1]) * reach_mask[-1]]
    broadcast_in_dim x9 -> x0, other arithmetic: 9.09 us -> none  [the longest x8 9.09 us: advance(): jnp.where(tail_keep[None], jnp.exp(tail_gaps), 0.0) * dt_block]
  transfers between devices with their start and end apart: 1 -> 0, of which waited for: 1 -> 0; matrix products, arithmetic and copies ran while one was open for 3% -> 0% of each run, Pallas kernels for 0% -> 0%
where the time goes in v1:
time: 57.7 us; the launch traced here: 57.3 us
  Pallas kernels  47.8 us (83%)
  local copies, waits for them, and re-layouts  9.52 us (16%)
    pallas_call x1, Pallas kernels, per_device(): pl.pallas_call(functools.partial(kernel_body, seq_n, xn, yn), out_shape=j...  47.8 us
    unnamed x21, local copies, waits for them, and re-layouts  9.52 us

profile of v1, /device:TPU:64, one launch (start us, length us, event | category | flops | bytes accessed | tf_op | source)
XLA Modules:
  0.0 57.3 jit_solution(9825528626426209115)
XLA Ops:
  0.0 0.0 copy-start
  0.0 1.2 %copy-done = bf16[1024,512]{1,0:T(8,128)(2,1)S(1)} copy-done((bf16[1024,512]{1,0:T(8,128)(2,1)S(1)}, bf16[1024,512]{1,0:T(8,128)(2,1)}, u32[]{:S(2)}) %copy-start) | copy-done | bytes 1048600
  1.2 0.0 copy-start.1
  1.2 1.2 %copy-done.1 = bf16[1024,512]{1,0:T(8,128)(2,1)S(1)} copy-done((bf16[1024,512]{1,0:T(8,128)(2,1)S(1)}, bf16[1024,512]{1,0:T(8,128)(2,1)}, u32[]{:S(2)}) %copy-start.1) | copy-done | bytes 1048600
  2.5 0.0 copy-start.2
  2.5 1.0 %copy-done.2 = bf16[4,512,128]{2,1,0:T(8,128)(2,1)S(1)} copy-done((bf16[4,512,128]{2,1,0:T(8,128)(2,1)S(1)}, bf16[4,512,128]{2,1,0:T(8,128)(2,1)}, u32[]{:S(2)}) %copy-start.2) | copy-done | bytes 524312
  3.5 0.0 copy-start.3
  3.5 1.0 %copy-done.3 = bf16[4,128,512]{2,1,0:T(8,128)(2,1)S(1)} copy-done((bf16[4,128,512]{2,1,0:T(8,128)(2,1)S(1)}, bf16[4,128,512]{2,1,0:T(8,128)(2,1)}, u32[]{:S(2)}) %copy-start.3) | copy-done | bytes 524312
  4.5 0.0 copy-start.4
  4.5 0.7 %copy-done.4 = f32[4,1024]{1,0:T(4,128)S(1)} copy-done((f32[4,1024]{1,0:T(4,128)S(1)}, f32[4,1024]{1,0:T(4,128)}, u32[]{:S(2)}) %copy-start.4) | copy-done | bytes 16408
  5.3 0.0 copy-start.5
  5.3 0.7 %copy-done.5 = f32[512]{0:T(512)S(1)} copy-done((f32[512]{0:T(512)S(1)}, f32[512]{0:T(512)}, u32[]{:S(2)}) %copy-start.5) | copy-done | bytes 2072
  5.9 0.0 copy-start.6
  5.9 0.7 %copy-done.6 = s32[6]{0:T(128)S(1)} copy-done((s32[6]{0:T(128)S(1)}, s32[6]{0:T(128)}, u32[]{:S(2)}) %copy-start.6) | copy-done | bytes 48
  6.6 0.0 copy-start.7
  6.6 0.7 %copy-done.7 = s32[6]{0:T(128)S(1)} copy-done((s32[6]{0:T(128)S(1)}, s32[6]{0:T(128)}, u32[]{:S(2)}) %copy-start.7) | copy-done | bytes 48
  7.2 0.0 copy-start.8
  7.2 0.7 %copy-done.8 = f32[4]{0:T(128)S(1)} copy-done((f32[4]{0:T(128)S(1)}, f32[4]{0:T(128)}, u32[]{:S(2)}) %copy-start.8) | copy-done | bytes 40
  7.9 0.0 copy-start.9
  7.9 0.7 %copy-done.9 = f32[4]{0:T(128)S(1)} copy-done((f32[4]{0:T(128)S(1)}, f32[4]{0:T(128)}, u32[]{:S(2)}) %copy-start.9) | copy-done | bytes 40
  8.6 47.8 %shard_map.118 = bf16[1024,512]{1,0:T(8,128)(2,1)S(1)} custom-call(s32[6]{0:T(128)S(1)} %copy-done.6, s32[6]{0:T(128)S(1)} %copy-done.7, f32[4]{0:T(128)S(1)} %copy-done.8, f32[4]{0:T(128)S(1)} %copy-done.9, f32[4,1024]{1,0:T(4,128)S(1)} %copy-done.4, f32[1,512]{1,0:T(1,128)S(1)} %bitcast.5, bf16[1024,512]{1,0:T(8,128)(2,1)S(1)} %copy-done, ...), custom_call_target="tpu_custom_call" | custom-call | tf_op jit(solution)/shard_map/pallas_call | solution.py:577
  56.4 1.0 %copy.14 = bf16[1024,512]{1,0:T(8,128)(2,1)} copy(bf16[1024,512]{1,0:T(8,128)(2,1)S(1)} %shard_map.118) | data formatting | bytes 2097152
Async XLA Ops:
  0.0 1.2 %copy-start = (bf16[1024,512]{1,0:T(8,128)(2,1)S(1)}, bf16[1024,512]{1,0:T(8,128)(2,1)}, u32[]{:S(2)}) copy-start(bf16[1024,512]{1,0:T(8,128)(2,1)} %x_hbm.1) | copy-start | bytes 3145732
  1.2 1.2 %copy-start.1 = (bf16[1024,512]{1,0:T(8,128)(2,1)S(1)}, bf16[1024,512]{1,0:T(8,128)(2,1)}, u32[]{:S(2)}) copy-start(bf16[1024,512]{1,0:T(8,128)(2,1)} %z_hbm.1) | copy-start | bytes 3145732
  2.5 1.0 %copy-start.2 = (bf16[4,512,128]{2,1,0:T(8,128)(2,1)S(1)}, bf16[4,512,128]{2,1,0:T(8,128)(2,1)}, u32[]{:S(2)}) copy-start(bf16[4,512,128]{2,1,0:T(8,128)(2,1)} %down_hbm.1) | copy-start | bytes 1572868
  3.5 1.0 %copy-start.3 = (bf16[4,128,512]{2,1,0:T(8,128)(2,1)S(1)}, bf16[4,128,512]{2,1,0:T(8,128)(2,1)}, u32[]{:S(2)}) copy-start(bf16[4,128,512]{2,1,0:T(8,128)(2,1)} %param.23) | copy-start | bytes 1572868
  4.5 0.7 %copy-start.4 = (f32[4,1024]{1,0:T(4,128)S(1)}, f32[4,1024]{1,0:T(4,128)}, u32[]{:S(2)}) copy-start(f32[4,1024]{1,0:T(4,128)} %dt_ref.1) | copy-start | bytes 49156
  5.3 0.7 %copy-start.5 = (f32[512]{0:T(512)S(1)}, f32[512]{0:T(512)}, u32[]{:S(2)}) copy-start(f32[512]{0:T(512)} %param.19) | copy-start | bytes 6148
  5.9 0.7 %copy-start.6 = (s32[6]{0:T(128)S(1)}, s32[6]{0:T(128)}, u32[]{:S(2)}) copy-start(s32[6]{0:T(128)} %doc_len.1) | copy-start | bytes 76
  6.6 0.7 %copy-start.7 = (s32[6]{0:T(128)S(1)}, s32[6]{0:T(128)}, u32[]{:S(2)}) copy-start(s32[6]{0:T(128)} %doc_lang.1) | copy-start | bytes 76
  7.2 0.7 %copy-start.8 = (f32[4]{0:T(128)S(1)}, f32[4]{0:T(128)}, u32[]{:S(2)}) copy-start(f32[4]{0:T(128)} %a_log.1) | copy-start | bytes 52
  7.9 0.7 %copy-start.9 = (f32[4]{0:T(128)S(1)}, f32[4]{0:T(128)}, u32[]{:S(2)}) copy-start(f32[4]{0:T(128)} %d_skip.1) | copy-start | bytes 52

commit v2 on v1

v2 whole, which is shorter than its diff:
```python
import functools

import jax
import jax.numpy as jnp
from jax import lax
from jax.experimental import pallas as pl
from jax.experimental.pallas import tpu as pltpu
from jax.sharding import PartitionSpec as P

SPACE_HEADS = 128
HEAD_DIM = 128
GROUPS = 8
L = 128
MESH = pl.DeviceIdType.MESH
F32 = jnp.float32
BF16 = jnp.bfloat16
HIGHEST = lax.Precision.HIGHEST


def nt(a, b, precision=None):
    return lax.dot_general(
        a, b, (((1,), (1,)), ((), ())), preferred_element_type=F32, precision=precision
    )


def mm(a, b, precision=None):
    return jnp.dot(a, b, preferred_element_type=F32, precision=precision)


def kernel_body(
    seq_n,
    xn,
    yn,
    doc_len_hbm,
    doc_lang_hbm,
    a_log_hbm,
    d_skip_hbm,
    dt_hbm,
    gain_hbm,
    x_hbm,
    z_hbm,
    b_hbm,
    c_hbm,
    down_hbm,
    up_hbm,
    out_hbm,
    doc_len,
    doc_lang,
    a_log,
    d_skip,
    dt_ref,
    gain_ref,
    gain_s,
    x_s,
    z_s,
    b_s,
    c_s,
    a_s,
    u_s,
    ypre,
    sz,
    g_s,
    out_s,
    sqs,
    pick_s,
    dt32,
    rowb,
    rows,
    wdev,
    colb,
    csel,
    bsel,
    bt,
    state,
    s_mine,
    s_part,
    d_mine,
    d_part,
    c_send,
    q1,
    dc_send,
    dq1,
    t_send,
    q2,
    h_mine,
    h_send,
    h_part,
    hb,
    pbuf,
    rx,
    qsum,
    ry,
    lbuf,
    ss_mine,
    ss_rx,
    ss_x,
    ss_ry,
    colscale,
    in_sem,
    out_sem,
    sa_sem,
    ra_sem,
    sx_sem,
    rx_sem,
    sy_sem,
    ry_sem,
    sgy_sem,
    rgy_sem,
    sgx_sem,
    rgx_sem,
    ssx_s,
    ssx_r,
    ssy_s,
    ssy_r,
):
    tok = x_s.shape[1]
    nc = tok // L
    nh = dt_ref.shape[0]
    qt = tok // xn
    pt = qt // yn
    rank = lax.axis_index("seq")
    hd = lax.axis_index("head")
    core = lax.rem(rank, 2)
    z = rank // 2
    nz = seq_n // 2
    mx = hd // yn
    my = lax.rem(hd, yn)
    group = hd * nh // (SPACE_HEADS // GROUPS)

    def seq_dev(dz):
        return (lax.rem(z + dz + nz, nz) * 2 + core, hd)

    partner = (z * 2 + 1 - core, hd)

    def x_dev(i):
        return (rank, lax.rem(mx + i, xn) * yn + my)

    def y_dev(i):
        return (rank, mx * yn + lax.rem(my + i, yn))

    chain = nz > 4
    peers = [partner]
    if chain:
        peers += [seq_dev(d) for d in (1, -1, 2, -2)]
    peers += [x_dev(i) for i in range(1, xn)]
    peers += [y_dev(i) for i in range(1, yn)]
    barrier = pltpu.get_barrier_semaphore()
    for peer in peers:
        pl.semaphore_signal(barrier, inc=1, device_id=peer, device_id_type=MESH)

    def load(src, dst, k):
        copy = pltpu.make_async_copy(src, dst, in_sem.at[k])
        copy.start()
        return copy

    small = [
        load(src, dst, 9 + k)
        for k, (src, dst) in enumerate(
            (
                (dt_hbm, dt_ref),
                (a_log_hbm, a_log),
                (doc_len_hbm, doc_len),
                (doc_lang_hbm, doc_lang),
                (d_skip_hbm, d_skip),
                (gain_hbm, gain_ref),
            )
        )
    ]
    def load_pair(src, dst, k):
        return [
            load(src.at[:, j, group // 2], dst.at[:, 2 * j : 2 * j + 2, :], k + j)
            for j in range(8)
        ]

    b_in = load_pair(b_hbm, b_s, 15)
    x_in = [load(x_hbm.at[:, pl.ds(k * 256, 256)], x_s.at[k], k) for k in range(2)]

    for copy in small:
        copy.wait()
    for c in range(nc):
        dt32[pl.ds(c * nh, nh), :] = dt_ref[:, pl.ds(c * L, L)]
    shape = (nc * nh, L)
    rid = lax.broadcasted_iota(jnp.int32, shape, 0)
    lane = lax.broadcasted_iota(jnp.int32, shape, 1)
    head_of = rid & (nh - 1)
    chunk_of = lax.shift_right_logical(rid, nh.bit_length() - 1)
    raw = dt32[...]
    dt = jnp.maximum(raw, 0.0) + jnp.log1p(jnp.exp(-jnp.abs(raw)))
    alog = jnp.full(shape, a_log[0], F32)
    for h in range(1, nh):
        alog = jnp.where(head_of == h, a_log[h], alog)
    ld = dt * -jnp.exp(alog)
    ki = lax.broadcasted_iota(jnp.int32, (L, L), 0)
    kj = lax.broadcasted_iota(jnp.int32, (L, L), 1)
    cum = mm(ld, (ki <= kj).astype(F32), HIGHEST)
    suf = mm(ld, (ki > kj).astype(F32), HIGHEST)
    tot = jnp.broadcast_to(jnp.sum(ld, axis=1, keepdims=True), shape)

    def down(v, k):
        return jnp.where(rid >= k, pltpu.roll(v, k, 0), 0.0)

    def up(v, k):
        return jnp.where(rid < nc * nh - k, pltpu.roll(v, nc * nh - k, 0), 0.0)

    pre, post = (down(tot, nh), up(tot, nh))
    step = nh
    while step < nc * nh:
        pre = pre + down(pre, step)
        post = post + up(post, step)
        step *= 2
    starts, first = ([], jnp.int32(0))
    for k in range(doc_len.shape[0]):
        starts.append(first)
        first = first + doc_len[k]
    base = rank * tok

    def docs(t):
        total = None
        for s in starts:
            one = (t >= s).astype(jnp.int32)
            total = one if total is None else total + one
        return total

    n_t = docs(base + chunk_of * L + lane)
    n_cs = docs(base + chunk_of * L - 1)
    n_ce = docs(base + chunk_of * L + (L - 1))
    n_bs = docs(base + 0 * chunk_of - 1)
    n_be = docs(base + 0 * chunk_of + (tok - 1))
    lang = jnp.zeros(shape, jnp.int32)
    for k in range(doc_lang.shape[0]):
        lang = jnp.where(n_t == k + 1, doc_lang[k], lang)

    def keep(cond, v):
        return jnp.where(cond, v, 0.0)

    carry = keep(n_t == n_cs, jnp.exp(cum))
    enter = keep(n_t == n_bs, jnp.exp(pre + cum))
    w_dev = keep(n_t == n_be, jnp.exp(suf + post)) * dt
    w_chunk = keep(n_t == n_ce, jnp.exp(suf)) * dt
    kept = keep(n_ce == n_cs, jnp.exp(tot))
    through = keep(n_be == n_bs, jnp.exp(pre + tot))
    n_f = n_t.astype(F32)
    lang_f = lang.astype(F32)
    for c in range(nc):
        own = slice(c * nh, (c + 1) * nh)
        for k, v in enumerate((cum, carry, enter)):
            rowb[c, k * nh : (k + 1) * nh, :] = v[own]
        rowb[c, 12:13, :] = n_f[c * nh : c * nh + 1]
        rowb[c, 13:14, :] = lang_f[c * nh : c * nh + 1]
        rowb[c, 14:16, :] = jnp.zeros((2, L), F32)
        for k, v in enumerate((cum, dt, w_chunk, kept)):
            rows[c, k * nh : (k + 1) * nh, :] = v[own]
        rows[c, 16:17, :] = n_f[c * nh : c * nh + 1]
        wdev[:, c * L : (c + 1) * L] = w_dev[own]
    for h in range(nh):
        r = (nc - 1) * nh + h
        d_mine[h] = jnp.broadcast_to(through[r : r + 1], (8, L))
    for k in range(2):
        gain_s[k] = jnp.broadcast_to(gain_ref[0:1, k * 256 : (k + 1) * 256], (8, 256))
    cols = jnp.transpose(rowb[...].reshape(nc * 16, L))
    for c in range(nc):
        colb[c * L : (c + 1) * L, 0:16] = cols[:, c * 16 : (c + 1) * 16]

    pr = lax.broadcasted_iota(jnp.int32, (L, L * 2), 0)
    pc = lax.broadcasted_iota(jnp.int32, (L, L * 2), 1)
    pick = (pc == pr * 2 + lax.rem(group, 2)).astype(BF16)
    for copy in b_in:
        copy.wait()
    c_in = load_pair(c_hbm, c_s, 23)
    z_in = [load(z_hbm.at[:, pl.ds(k * 256, 256)], z_s.at[k], 2 + k) for k in range(2)]
    a_in = [
        load(
            down_hbm.at[k % 4, pl.ds(k // 4 * 256, 256), :],
            a_s.at[k // 4, :, pl.ds(k % 4 * 128, 128)],
            31 + k,
        )
        for k in range(8)
    ]
    u_in = load(up_hbm, u_s, 8)
    for c in range(nc):
        part = mm(pick, b_s[c * 16 : (c + 1) * 16].reshape(2 * L, 128)).astype(BF16)
        bsel[c * L : (c + 1) * L, :] = part
        bt[:, c * L : (c + 1) * L] = jnp.transpose(part)
    pl.semaphore_wait(barrier, len(peers))

    def send(src, dst, s_sem, r_sem, dev):
        copy = pltpu.make_async_remote_copy(
            src_ref=src, dst_ref=dst, send_sem=s_sem, recv_sem=r_sem,
            device_id=dev, device_id_type=MESH,
        )
        copy.start()
        return copy

    pair = [send(d_mine, d_part, sa_sem.at[0], ra_sem.at[0], partner)]
    for copy in x_in:
        copy.wait()
    other = 1 - core
    for k in range(nh):
        half = other if k < 2 else core
        j = k % 2
        h = half * 2 + j
        lhs = bt[...] * wdev[pl.ds(h, 1), :].astype(BF16)
        s_mine[h] = mm(lhs, x_s[half, :, j * 128 : (j + 1) * 128])
        pair.append(send(s_mine.at[h], s_part.at[h], sa_sem.at[1 + k], ra_sem.at[1 + k], partner))

    for copy in c_in:
        copy.wait()
    for c in range(nc):
        part = mm(pick, c_s[c * 16 : (c + 1) * 16].reshape(2 * L, 128))
        csel[c * L : (c + 1) * L, :] = part.astype(BF16)

    is_second = core == 1
    mine = [core * 2 + j for j in range(2)]
    pair[0].wait_recv()
    ring, chip_d = ([], [])
    if chain:
        for j in range(2):
            chip_d.append(d_mine[mine[j]][0:1] * d_part[mine[j]][0:1])
            dc_send[j] = jnp.broadcast_to(chip_d[j], (8, L))
        ring.append(send(dc_send, dq1, sa_sem.at[5], ra_sem.at[5], seq_dev(1)))
        for j in range(2):
            pair[1 + j].wait_recv()
            sm, sp = (s_mine[mine[j]], s_part[mine[j]])
            earlier = jnp.where(is_second, sp, sm)
            latter = jnp.where(is_second, sm, sp)
            d_latter = jnp.where(is_second, d_mine[mine[j]][0:1], d_part[mine[j]][0:1])
            chip_s = d_latter * earlier + latter
            h_mine[j] = chip_s
            c_send[j] = chip_s.astype(BF16)
            ring.append(
                send(c_send.at[j], q1.at[j], sa_sem.at[6 + j], ra_sem.at[6 + j], seq_dev(1))
            )
    else:
        for j in range(2):
            pair[1 + j].wait_recv()

    state[...] = jnp.zeros_like(state)
    lower = ki >= kj

    def chunk(c):
        at = pl.multiple_of(c * L, L)
        col = colb[pl.ds(at, L), :]
        row = rows[c]
        cc = csel[pl.ds(at, L), :]
        gram = nt(cc, bsel[pl.ds(at, L), :])
        same = col[:, 12:13] == row[16:17]
        gram = jnp.where(same & lower, gram, 0.0)
        cf = cc.astype(F32)
        btc = bt[:, pl.ds(at, L)]
        for h in range(nh):
            half, hs = (h // 2, slice(h % 2 * 128, (h % 2 + 1) * 128))
            gap = jnp.minimum(col[:, h : h + 1] - row[h : h + 1], 0.0)
            w = (gram * jnp.exp(gap) * row[nh + h : nh + h + 1]).astype(BF16)
            xh = x_s[half, pl.ds(at, L), hs]
            st = state[h]
            cw = (cf * col[:, nh + h : nh + h + 1]).astype(BF16)
            y = mm(w, xh) + mm(cw, st.astype(BF16)) + d_skip[h] * xh.astype(F32)
            ypre[half, pl.ds(at, L), hs] = y
            new = btc * row[2 * nh + h : 2 * nh + h + 1].astype(BF16)
            state[h] = st * row[3 * nh + h : 3 * nh + h + 1] + mm(new, xh)

    def chunks(i, carry_in):
        chunk(2 * i)
        chunk(2 * i + 1)
        return carry_in

    def silu(c, carry_in):
        at = pl.multiple_of(c * L, L)
        for half in range(2):
            v = z_s[half, pl.ds(at, L), :].astype(F32)
            sz[half, pl.ds(at, L), :] = v / (1.0 + jnp.exp(-v))
        return carry_in

    cut = nc // 4
    lax.fori_loop(0, cut, chunks, 0)

    far = []
    if chain:
        ring[0].wait_recv()
        for j in range(2):
            ring[1 + j].wait_recv()
            from1 = jnp.where(z >= 1, q1[j].astype(F32), 0.0)
            t_send[j] = (h_mine[j] + chip_d[j] * from1).astype(BF16)
            far.append(
                send(t_send.at[j], q2.at[j], sa_sem.at[8 + j], ra_sem.at[8 + j], seq_dev(2))
            )
    for copy in z_in:
        copy.wait()
    lax.fori_loop(cut, nc // 2, chunks, 0)
    lax.fori_loop(0, nc, silu, 0)
    for copy in a_in:
        copy.wait()
    pair[3].wait_recv()
    pair[4].wait_recv()
    for copy in pair + ring:
        copy.wait_send()

    def entering(inc, h):
        second = d_part[h][0:1] * inc + s_part[h]
        return jnp.where(is_second, second, inc).astype(BF16)

    back = []
    for j in range(2):
        js = slice(j * 128, (j + 1) * 128)
        if chain:
            far[j].wait_recv()
            from1 = jnp.where(z >= 1, q1[j].astype(F32), 0.0)
            from2 = jnp.where(z >= 2, q2[j].astype(F32), 0.0)
            inc = from1 + dq1[j][0:1] * from2
            h_send[j] = inc
            back.append(
                send(h_send.at[j], h_part.at[j], sa_sem.at[10 + j], ra_sem.at[10 + j], partner)
            )
        else:
            inc = jnp.zeros((128, 128), F32)
        hb[core, :, js] = entering(inc, mine[j])

    one8 = jnp.ones((8, L), BF16)

    def gate(q, half, last):
        at = q * qt if isinstance(q, int) else pl.multiple_of(q * qt, qt)
        here = pl.ds(at, qt)
        col = colb[here, :]
        cc = csel[here, :]
        sq = sqs[here, :] if last else None
        picked = pick_s[here, :] if last else None
        for j in range(2):
            js = slice(j * 128, (j + 1) * 128)
            lo = col[:, 2 * nh + j : 2 * nh + j + 1]
            hi = col[:, 2 * nh + 2 + j : 2 * nh + 3 + j]
            ent = mm(cc, hb[half, :, js]) * jnp.where(half == 1, hi, lo)
            gated = (ypre[half, here, js] + ent) * sz[half, here, js]
            sq = gated * gated if sq is None else sq + gated * gated
            g_s[half, here, js] = (gated * gain_s[half, 0:1, js]).astype(BF16)
        lg = col[:, 13:14]
        for k in range(0, 4, 2):
            two = mm(g_s[half, here, :], a_s[half, :, k * 128 : (k + 2) * 128])
            for j in range(2):
                one = jnp.where(lg == float(k + j), two[:, j * 128 : (j + 1) * 128], 0.0)
                picked = one if picked is None else picked + one
        if last:
            sums = nt(one8, sq.astype(BF16))
            for i in range(qt // L):
                ss_mine[pl.ds(q * (qt // L) + i, 1), :] = sums[0:1, i * L : (i + 1) * L]
            pbuf[q] = picked.astype(BF16)
        else:
            sqs[here, :] = sq
            pick_s[here, :] = picked

    for q in range(xn):
        gate(q, core, False)
    for j in range(2):
        if chain:
            back[j].wait_recv()
            inc = h_part[j]
        else:
            inc = jnp.zeros((128, 128), F32)
        hb[other, :, j * 128 : (j + 1) * 128] = entering(inc, other * 2 + j)
    for copy in back + far:
        copy.wait_send()
    sends = []
    order = sorted(range(1, xn), key=lambda i: -min(i, xn - i))
    for i in order:
        q = lax.rem(mx + i, xn)
        gate(q, other, True)
        sends.append(send(pbuf.at[q], rx.at[mx], sx_sem.at[i], rx_sem.at[mx], x_dev(i)))
    gate(mx, other, True)
    for i in order:
        sends.append(send(ss_mine, ss_rx.at[mx], ssx_s.at[i], ssx_r.at[mx], x_dev(i)))

    def arrived(dst, sem):
        pltpu.make_async_remote_copy(
            src_ref=dst, dst_ref=dst, send_sem=in_sem.at[0], recv_sem=sem,
            device_id=partner, device_id_type=MESH,
        ).wait_recv()

    total = pbuf[mx].astype(F32)
    for i in order[::-1]:
        src = lax.rem(mx + i, xn)
        arrived(rx.at[src], rx_sem.at[src])
        total = total + rx[src].astype(F32)
    qsum[...] = total.astype(BF16).reshape(qsum.shape)
    y_order = sorted(range(1, yn), key=lambda i: -min(i, yn - i))
    for i in y_order:
        p = lax.rem(my + i, yn)
        sends.append(send(qsum.at[p], ry.at[my], sy_sem.at[i], ry_sem.at[my], y_dev(i)))
    ss = ss_mine[...]
    for i in order[::-1]:
        src = lax.rem(mx + i, xn)
        arrived(ss_rx.at[src], ssx_r.at[src])
        ss = ss + ss_rx[src]
    ss_x[...] = ss
    for i in y_order:
        sends.append(send(ss_x, ss_ry.at[my], ssy_s.at[i], ssy_r.at[my], y_dev(i)))
    piece = qsum[my].astype(F32)
    for i in y_order[::-1]:
        src = lax.rem(my + i, yn)
        arrived(ry.at[src], ry_sem.at[src])
        piece = piece + ry[src].astype(F32)
    lbuf[mx, my] = piece.astype(BF16)
    for i in y_order:
        sends.append(send(lbuf.at[mx, my], lbuf.at[mx, my], sgy_sem.at[i], rgy_sem.at[my], y_dev(i)))

    def forward(p, k):
        for i in order:
            sends.append(
                send(lbuf.at[mx, p], lbuf.at[mx, p], sgx_sem.at[i, k], rgx_sem.at[mx], x_dev(i))
            )

    forward(my, 0)

    for i in y_order[::-1]:
        src = lax.rem(my + i, yn)
        arrived(ss_ry.at[src], ssy_r.at[src])
        ss = ss + ss_ry[src]
    scale = lax.rsqrt(ss / (SPACE_HEADS * HEAD_DIM) + 1e-05)
    eye = ki == kj
    for c in range(nc):
        spread = jnp.broadcast_to(scale[c : c + 1], (L, L))
        one = jnp.sum(jnp.where(eye, spread, 0.0), axis=1, keepdims=True)
        colscale[c * L : (c + 1) * L, :] = jnp.broadcast_to(one, (L, L))

    for i in y_order[::-1]:
        p = lax.rem(my + i, yn)
        arrived(lbuf.at[mx, p], rgy_sem.at[p])
        forward(p, i)

    u_in.wait()

    def finish(q):
        at = pl.multiple_of(q * qt, qt)
        here = pl.ds(at, qt)
        lg = colb[here, 13:14]
        low = lbuf[q].reshape(qt, 128)
        sel = jnp.concatenate(
            [jnp.where(lg == float(k), low, jnp.zeros_like(low)) for k in range(4)], axis=1
        )
        scl = colscale[here, :]
        for h in range(0, nh, 2):
            lift = mm(sel, u_s[:, h * 128 : (h + 2) * 128])
            for j in range(2):
                hs = slice((h + j) * 128, (h + j + 1) * 128)
                val = g_s[h // 2, here, j * 128 : (j + 1) * 128].astype(F32) + lift[:, j * 128 : (j + 1) * 128]
                out_s[here, hs] = (val * scl).astype(BF16)
        copy = pltpu.make_async_copy(
            out_s.at[here, :], out_hbm.at[here, :], out_sem.at[q]
        )
        copy.start()
        return copy

    outs = [finish(mx)]
    for i in order[::-1]:
        q = lax.rem(mx + i, xn)
        arrived(lbuf.at[q], rgx_sem.at[q])
        outs.append(finish(q))
    for copy in sends:
        copy.wait_send()
    for copy in outs:
        copy.wait()


def per_device(seq_n, xn, yn, x_in, z_gate, b_input, c_input, dt_raw, a_log, d_skip, norm_gain,
               doc_lengths, doc_lang, adapt_down, adapt_up):
    tok, feat = x_in.shape
    nh = dt_raw.shape[0]
    nc = tok // L
    qt = tok // xn
    pt = qt // yn
    half = feat // 2
    dma = pltpu.SemaphoreType.DMA
    vm = pltpu.VMEM
    scratch = [
        pltpu.SMEM(doc_lengths.shape, jnp.int32),
        pltpu.SMEM(doc_lang.shape, jnp.int32),
        pltpu.SMEM((nh,), F32),
        pltpu.SMEM((nh,), F32),
        vm((nh, tok), F32),
        vm((1, feat), F32),
        vm((2, 8, half), F32),
        vm((2, tok, half), BF16),
        vm((2, tok, half), BF16),
        vm((tok // 8, 16, 128), BF16),
        vm((tok // 8, 16, 128), BF16),
        vm((2, half, 512), BF16),
        vm((512, feat), BF16),
        vm((2, tok, half), F32),
        vm((2, tok, half), F32),
        vm((2, tok, half), BF16),
        vm((tok, feat), BF16),
        vm((tok, L), F32),
        vm((tok, L), F32),
        vm((nc * nh, L), F32),
        vm((nc, 16, L), F32),
        vm((nc, 24, L), F32),
        vm((nh, tok), F32),
        vm((tok, L), F32),
        vm((tok, L), BF16),
        vm((tok, L), BF16),
        vm((L, tok), BF16),
        vm((nh, 128, 128), F32),
        vm((nh, 128, 128), F32),
        vm((nh, 128, 128), F32),
        vm((nh, 8, L), F32),
        vm((nh, 8, L), F32),
        vm((2, 128, 128), BF16),
        vm((2, 128, 128), BF16),
        vm((2, 8, L), F32),
        vm((2, 8, L), F32),
        vm((2, 128, 128), BF16),
        vm((2, 128, 128), BF16),
        vm((2, 128, 128), F32),
        vm((2, 128, 128), F32),
        vm((2, 128, 128), F32),
        vm((2, 128, half), BF16),
        vm((xn, qt, 128), BF16),
        vm((xn, qt, 128), BF16),
        vm((yn, pt, 128), BF16),
        vm((yn, pt, 128), BF16),
        vm((xn, yn, pt, 128), BF16),
        vm((nc, L), F32),
        vm((xn, nc, L), F32),
        vm((nc, L), F32),
        vm((yn, nc, L), F32),
        vm((tok, L), F32),
        dma((39,)),
        dma((xn,)),
        dma((12,)),
        dma((12,)),
        dma((xn,)),
        dma((xn,)),
        dma((yn,)),
        dma((yn,)),
        dma((yn,)),
        dma((yn,)),
        dma((xn, yn)),
        dma((xn,)),
        dma((xn,)),
        dma((xn,)),
        dma((yn,)),
        dma((yn,)),
    ]
    hbm = pl.BlockSpec(memory_space=pltpu.HBM)
    return pl.pallas_call(
        functools.partial(kernel_body, seq_n, xn, yn),
        out_shape=jax.ShapeDtypeStruct((tok, feat), BF16),
        in_specs=[hbm] * 12,
        out_specs=hbm,
        scratch_shapes=scratch,
        compiler_params=pltpu.CompilerParams(
            collective_id=0, has_side_effects=True, vmem_limit_bytes=60 * 1024 * 1024
        ),
    )(
        doc_lengths,
        doc_lang,
        a_log,
        d_skip,
        dt_raw,
        norm_gain.reshape(1, feat),
        x_in,
        z_gate,
        b_input.reshape(tok // 8, 8, GROUPS // 2, 2, 128),
        c_input.reshape(tok // 8, 8, GROUPS // 2, 2, 128),
        adapt_down,
        adapt_up.reshape(512, feat),
    )


def solution(mesh):
    seq_n, head_n = mesh.shape["seq"], mesh.shape["head"]
    xn = 4 if head_n == 32 else min(2, head_n)
    placed = (
        P("seq", "head"),
        P("seq", "head"),
        P("seq", None, None),
        P("seq", None, None),
        P("head", "seq"),
        P("head"),
        P("head"),
        P("head"),
        P(),
        P(),
        P(None, "head", None),
        P(None, None, "head"),
    )
    return jax.shard_map(
        functools.partial(per_device, seq_n, xn, head_n // xn),
        mesh=mesh, in_specs=placed, out_specs=P("seq", "head"), check_vma=False,
    )
```

time: 57.7 us -> 47.9 us (0.83)
  local copies, waits for them, and re-layouts: 9.52 us -> 2.26 us
  Pallas kernels: 47.8 us -> 45.4 us
    unnamed x21 -> x1, local copies, waits for them, and re-layouts: 9.52 us -> 2.26 us
    pallas_call x1, Pallas kernels: 47.8 us -> 45.4 us  [per_device(): pl.pallas_call(functools.partial(kernel_body, seq_n, xn, yn), out_shape=j...]
where the time goes in v2:
time: 47.9 us; the launch traced here: 47.7 us
  Pallas kernels  45.4 us (95%)
  local copies, waits for them, and re-layouts  2.26 us (5%)
    pallas_call x1, Pallas kernels, per_device(): pl.pallas_call(functools.partial(kernel_body, seq_n, xn, yn), out_shape=j...  45.4 us
    unnamed x1, local copies, waits for them, and re-layouts  2.26 us

profile of v2, /device:TPU:64, one launch (start us, length us, event | category | flops | bytes accessed | tf_op | source)
XLA Modules:
  0.0 47.7 jit_solution(13505617829996729249)
XLA Ops:
  0.0 45.4 %shard_map.118 = bf16[1024,512]{1,0:T(8,128)(2,1)} custom-call(s32[6]{0:T(128)} %doc_len_hbm.1, s32[6]{0:T(128)} %doc_lang_hbm.1, f32[4]{0:T(128)} %a_log_hbm.1, f32[4]{0:T(128)} %d_skip_hbm.1, f32[4,1024]{1,0:T(4,128)} %dt_hbm.1, f32[1,512]{1,0:T(1,128)} %bitcast.7, bf16[1024,512]{1,0:T(8,128)(2,1)} %x_hbm.1, bf16[1024,512]{1,0:T(8,128)(2,1)} %z_hbm.1, ...), custom_call_target="tpu_custom_call" | custom-call | tf_op jit(solution)/shard_map/pallas_call | solution.py:643
  45.4 2.3 %copy.14 = bf16[1024,512]{1,0:T(8,128)(2,1)} copy(bf16[1024,512]{1,0:T(8,128)(2,1)} %shard_map.118) | data formatting | bytes 2097152

commit v3 on v2

--- a/solution.py
+++ b/solution.py
@@ -112,6 +112,7 @@
     ssx_r,
     ssy_s,
     ssy_r,
+    ready,
 ):
     tok = x_s.shape[1]
     nc = tok // L
@@ -139,14 +140,20 @@
         return (rank, mx * yn + lax.rem(my + i, yn))
 
     chain = nz > 4
+    has = {1: z >= 1, 2: z >= 2}
+    feeds = {1: z < nz - 1, 2: z < nz - 2}
     peers = [partner]
-    if chain:
-        peers += [seq_dev(d) for d in (1, -1, 2, -2)]
     peers += [x_dev(i) for i in range(1, xn)]
     peers += [y_dev(i) for i in range(1, yn)]
     barrier = pltpu.get_barrier_semaphore()
     for peer in peers:
         pl.semaphore_signal(barrier, inc=1, device_id=peer, device_id_type=MESH)
+    if chain:
+        for d in (1, 2):
+
+            @pl.when(feeds[d])
+            def _():
+                pl.semaphore_signal(barrier, inc=1, device_id=seq_dev(d), device_id_type=MESH)
 
     def load(src, dst, k):
         copy = pltpu.make_async_copy(src, dst, in_sem.at[k])
@@ -281,13 +288,24 @@
         part = mm(pick, b_s[c * 16 : (c + 1) * 16].reshape(2 * L, 128)).astype(BF16)
         bsel[c * L : (c + 1) * L, :] = part
         bt[:, c * L : (c + 1) * L] = jnp.transpose(part)
-    pl.semaphore_wait(barrier, len(peers))
-
-    def send(src, dst, s_sem, r_sem, dev):
-        copy = pltpu.make_async_remote_copy(
+    pl.semaphore_wait(barrier, len(peers) + (jnp.minimum(z, 2) if chain else 0))
+    if chain:
+        for d in (1, 2):
+
+            @pl.when(has[d])
+            def _():
+                pl.semaphore_signal(
+                    ready.at[d - 1], inc=1, device_id=seq_dev(-d), device_id_type=MESH
+                )
+
+    def remote(src, dst, s_sem, r_sem, dev):
+        return pltpu.make_async_remote_copy(
             src_ref=src, dst_ref=dst, send_sem=s_sem, recv_sem=r_sem,
             device_id=dev, device_id_type=MESH,
         )
+
+    def send(src, dst, s_sem, r_sem, dev):
+        copy = remote(src, dst, s_sem, r_sem, dev)
         copy.start()
         return copy
 
@@ -312,12 +330,28 @@
     is_second = core == 1
     mine = [core * 2 + j for j in range(2)]
     pair[0].wait_recv()
-    ring, chip_d = ([], [])
+    ring, far, chip_d = ([], [], [])
     if chain:
         for j in range(2):
             chip_d.append(d_mine[mine[j]][0:1] * d_part[mine[j]][0:1])
             dc_send[j] = jnp.broadcast_to(chip_d[j], (8, L))
-        ring.append(send(dc_send, dq1, sa_sem.at[5], ra_sem.at[5], seq_dev(1)))
+        ring = [remote(dc_send, dq1, sa_sem.at[5], ra_sem.at[5], seq_dev(1))]
+        for j in range(2):
+            ring.append(
+                remote(c_send.at[j], q1.at[j], sa_sem.at[6 + j], ra_sem.at[6 + j], seq_dev(1))
+            )
+            far.append(
+                remote(t_send.at[j], q2.at[j], sa_sem.at[8 + j], ra_sem.at[8 + j], seq_dev(2))
+            )
+
+        late = z == 2
+        early = feeds[1] & jnp.logical_not(late)
+
+        @pl.when(early)
+        def _():
+            pl.semaphore_wait(ready.at[0], 1)
+            ring[0].start()
+
         for j in range(2):
             pair[1 + j].wait_recv()
             sm, sp = (s_mine[mine[j]], s_part[mine[j]])
@@ -327,9 +361,18 @@
             chip_s = d_latter * earlier + latter
             h_mine[j] = chip_s
             c_send[j] = chip_s.astype(BF16)
-            ring.append(
-                send(c_send.at[j], q1.at[j], sa_sem.at[6 + j], ra_sem.at[6 + j], seq_dev(1))
-            )
+
+            @pl.when(early)
+            def _():
+                ring[1 + j].start()
+
+        @pl.when(z == 0)
+        def _():
+            pl.semaphore_wait(ready.at[1], 1)
+            for j in range(2):
+                t_send[j] = c_send[j]
+                far[j].start()
+
     else:
         for j in range(2):
             pair[1 + j].wait_recv()
@@ -374,16 +417,30 @@
     cut = nc // 4
     lax.fori_loop(0, cut, chunks, 0)
 
-    far = []
     if chain:
-        ring[0].wait_recv()
-        for j in range(2):
-            ring[1 + j].wait_recv()
-            from1 = jnp.where(z >= 1, q1[j].astype(F32), 0.0)
-            t_send[j] = (h_mine[j] + chip_d[j] * from1).astype(BF16)
-            far.append(
-                send(t_send.at[j], q2.at[j], sa_sem.at[8 + j], ra_sem.at[8 + j], seq_dev(2))
-            )
+
+        @pl.when(late)
+        def _():
+            pl.semaphore_wait(ready.at[0], 1)
+            for copy in ring:
+                copy.start()
+
+        @pl.when(has[1])
+        def _():
+            ring[0].wait_recv()
+            for j in range(2):
+                ring[1 + j].wait_recv()
+                t_send[j] = (h_mine[j] + chip_d[j] * q1[j].astype(F32)).astype(BF16)
+                if j == 0:
+
+                    @pl.when(feeds[2])
+                    def _():
+                        pl.semaphore_wait(ready.at[1], 1)
+
+                @pl.when(feeds[2])
+                def _():
+                    far[j].start()
+
     for copy in z_in:
         copy.wait()
     lax.fori_loop(cut, nc // 2, chunks, 0)
@@ -392,8 +449,15 @@
         copy.wait()
     pair[3].wait_recv()
     pair[4].wait_recv()
-    for copy in pair + ring:
+    for copy in pair:
         copy.wait_send()
+    if chain:
+
+        @pl.when(feeds[1])
+        def _():
+            for copy in ring:
+                copy.wait_send()
+
 
     def entering(inc, h):
         second = d_part[h][0:1] * inc + s_part[h]
@@ -403,11 +467,21 @@
     for j in range(2):
         js = slice(j * 128, (j + 1) * 128)
         if chain:
-            far[j].wait_recv()
-            from1 = jnp.where(z >= 1, q1[j].astype(F32), 0.0)
-            from2 = jnp.where(z >= 2, q2[j].astype(F32), 0.0)
-            inc = from1 + dq1[j][0:1] * from2
-            h_send[j] = inc
+
+            @pl.when(z == 0)
+            def _():
+                h_send[j] = jnp.zeros((128, 128), F32)
+
+            @pl.when(z == 1)
+            def _():
+                h_send[j] = q1[j].astype(F32)
+
+            @pl.when(has[2])
+            def _():
+                far[j].wait_recv()
+                h_send[j] = q1[j].astype(F32) + dq1[j][0:1] * q2[j].astype(F32)
+
+            inc = h_send[j]
             back.append(
                 send(h_send.at[j], h_part.at[j], sa_sem.at[10 + j], ra_sem.at[10 + j], partner)
             )
@@ -456,8 +530,15 @@
         else:
             inc = jnp.zeros((128, 128), F32)
         hb[other, :, j * 128 : (j + 1) * 128] = entering(inc, other * 2 + j)
-    for copy in back + far:
+    for copy in back:
         copy.wait_send()
+    if chain:
+
+        @pl.when(feeds[2])
+        def _():
+            for copy in far:
+                copy.wait_send()
+
     sends = []
     order = sorted(range(1, xn), key=lambda i: -min(i, xn - i))
     for i in order:
@@ -638,18 +719,20 @@
         dma((xn,)),
         dma((yn,)),
         dma((yn,)),
+        pltpu.SemaphoreType.REGULAR((2,)),
     ]
     hbm = pl.BlockSpec(memory_space=pltpu.HBM)
-    return pl.pallas_call(
+    call = pl.pallas_call(
         functools.partial(kernel_body, seq_n, xn, yn),
         out_shape=jax.ShapeDtypeStruct((tok, feat), BF16),
         in_specs=[hbm] * 12,
-        out_specs=hbm,
+        out_specs=pl.BlockSpec(memory_space=pl.ANY),
         scratch_shapes=scratch,
         compiler_params=pltpu.CompilerParams(
-            collective_id=0, has_side_effects=True, vmem_limit_bytes=60 * 1024 * 1024
+            collective_id=0, has_side_effects=True, vmem_limit_bytes=40 * 1024 * 1024
         ),
-    )(
+    )
+    operands = (
         doc_lengths,
         doc_lang,
         a_log,
@@ -663,6 +746,7 @@
         adapt_down,
         adapt_up.reshape(512, feat),
     )
+    return call(*[pltpu.with_memory_space_constraint(v, pltpu.HBM) for v in operands])
 
 
 def solution(mesh):

time: 47.9 us -> 41 us (0.86)
  the two profiles are of different devices: /device:TPU:64 before, /device:TPU:384 now
where the time goes in v3:
time: 41 us; the launch traced here: 40.8 us
  Pallas kernels  39.8 us (97%)
  local copies, waits for them, and re-layouts  0.97 us (2%)
    pallas_call x1, Pallas kernels, per_device(): call(*[pltpu.with_memory_space_constraint(v, pltpu.HBM) for v in operands])  39.8 us
    unnamed x1, local copies, waits for them, and re-layouts  0.97 us

profile of v3, /device:TPU:384, one launch (start us, length us, event | category | flops | bytes accessed | tf_op | source)
XLA Modules:
  0.0 40.8 jit_solution(11901218680488237116)
XLA Ops:
  0.0 39.8 %shard_map.118 = bf16[1024,512]{1,0:T(8,128)(2,1)S(1)} custom-call(s32[6]{0:T(128)} %doc_len_hbm.1, s32[6]{0:T(128)} %doc_lang_hbm.1, f32[4]{0:T(128)} %a_log_hbm.1, f32[4]{0:T(128)} %d_skip_hbm.1, f32[4,1024]{1,0:T(4,128)} %dt_hbm.1, f32[1,512]{1,0:T(1,128)} %bitcast.7, bf16[1024,512]{1,0:T(8,128)(2,1)} %x_hbm.1, bf16[1024,512]{1,0:T(8,128)(2,1)} %z_hbm.1, ...), custom_call_target="tpu_custom_call" | custom-call | tf_op jit(solution)/shard_map/pallas_call | solution.py:749
  39.8 1.0 %copy.14 = bf16[1024,512]{1,0:T(8,128)(2,1)} copy(bf16[1024,512]{1,0:T(8,128)(2,1)S(1)} %shard_map.118) | data formatting | bytes 2097152

commit v4 on v3

--- a/solution.py
+++ b/solution.py
@@ -43,7 +43,7 @@
     c_hbm,
     down_hbm,
     up_hbm,
-    out_hbm,
+    out_ref,
     doc_len,
     doc_lang,
     a_log,
@@ -60,7 +60,6 @@
     ypre,
     sz,
     g_s,
-    out_s,
     sqs,
     pick_s,
     dt32,
@@ -97,7 +96,6 @@
     ss_ry,
     colscale,
     in_sem,
-    out_sem,
     sa_sem,
     ra_sem,
     sx_sem,
@@ -145,16 +143,6 @@
     peers = [partner]
     peers += [x_dev(i) for i in range(1, xn)]
     peers += [y_dev(i) for i in range(1, yn)]
-    barrier = pltpu.get_barrier_semaphore()
-    for peer in peers:
-        pl.semaphore_signal(barrier, inc=1, device_id=peer, device_id_type=MESH)
-    if chain:
-        for d in (1, 2):
-
-            @pl.when(feeds[d])
-            def _():
-                pl.semaphore_signal(barrier, inc=1, device_id=seq_dev(d), device_id_type=MESH)
-
     def load(src, dst, k):
         copy = pltpu.make_async_copy(src, dst, in_sem.at[k])
         copy.start()
@@ -180,6 +168,16 @@
         ]
 
     b_in = load_pair(b_hbm, b_s, 15)
+    barrier = pltpu.get_barrier_semaphore()
+    for peer in peers:
+        pl.semaphore_signal(barrier, inc=1, device_id=peer, device_id_type=MESH)
+    if chain:
+        for d in (1, 2):
+
+            @pl.when(feeds[d])
+            def _():
+                pl.semaphore_signal(barrier, inc=1, device_id=seq_dev(d), device_id_type=MESH)
+
     x_in = [load(x_hbm.at[:, pl.ds(k * 256, 256)], x_s.at[k], k) for k in range(2)]
 
     for copy in small:
@@ -328,55 +326,6 @@
         csel[c * L : (c + 1) * L, :] = part.astype(BF16)
 
     is_second = core == 1
-    mine = [core * 2 + j for j in range(2)]
-    pair[0].wait_recv()
-    ring, far, chip_d = ([], [], [])
-    if chain:
-        for j in range(2):
-            chip_d.append(d_mine[mine[j]][0:1] * d_part[mine[j]][0:1])
-            dc_send[j] = jnp.broadcast_to(chip_d[j], (8, L))
-        ring = [remote(dc_send, dq1, sa_sem.at[5], ra_sem.at[5], seq_dev(1))]
-        for j in range(2):
-            ring.append(
-                remote(c_send.at[j], q1.at[j], sa_sem.at[6 + j], ra_sem.at[6 + j], seq_dev(1))
-            )
-            far.append(
-                remote(t_send.at[j], q2.at[j], sa_sem.at[8 + j], ra_sem.at[8 + j], seq_dev(2))
-            )
-
-        late = z == 2
-        early = feeds[1] & jnp.logical_not(late)
-
-        @pl.when(early)
-        def _():
-            pl.semaphore_wait(ready.at[0], 1)
-            ring[0].start()
-
-        for j in range(2):
-            pair[1 + j].wait_recv()
-            sm, sp = (s_mine[mine[j]], s_part[mine[j]])
-            earlier = jnp.where(is_second, sp, sm)
-            latter = jnp.where(is_second, sm, sp)
-            d_latter = jnp.where(is_second, d_mine[mine[j]][0:1], d_part[mine[j]][0:1])
-            chip_s = d_latter * earlier + latter
-            h_mine[j] = chip_s
-            c_send[j] = chip_s.astype(BF16)
-
-            @pl.when(early)
-            def _():
-                ring[1 + j].start()
-
-        @pl.when(z == 0)
-        def _():
-            pl.semaphore_wait(ready.at[1], 1)
-            for j in range(2):
-                t_send[j] = c_send[j]
-                far[j].start()
-
-    else:
-        for j in range(2):
-            pair[1 + j].wait_recv()
-
     state[...] = jnp.zeros_like(state)
     lower = ki >= kj
 
@@ -415,7 +364,72 @@
         return carry_in
 
     cut = nc // 4
-    lax.fori_loop(0, cut, chunks, 0)
+
+    @pl.when(core == 0)
+    def _():
+        lax.fori_loop(0, cut, chunks, 0)
+
+    mine = [core * 2 + j for j in range(2)]
+    pair[0].wait_recv()
+    ring, far, chip_d = ([], [], [])
+    if chain:
+        for j in range(2):
+            chip_d.append(d_mine[mine[j]][0:1] * d_part[mine[j]][0:1])
+            dc_send[j] = jnp.broadcast_to(chip_d[j], (8, L))
+        ring = [remote(dc_send, dq1, sa_sem.at[5], ra_sem.at[5], seq_dev(1))]
+        for j in range(2):
+            ring.append(
+                remote(c_send.at[j], q1.at[j], sa_sem.at[6 + j], ra_sem.at[6 + j], seq_dev(1))
+            )
+            far.append(
+                remote(t_send.at[j], q2.at[j], sa_sem.at[8 + j], ra_sem.at[8 + j], seq_dev(2))
+            )
+
+        late = z == 2
+        early = feeds[1] & jnp.logical_not(late)
+
+        for j in range(2):
+            pair[1 + j].wait_recv()
+            sm, sp = (s_mine[mine[j]], s_part[mine[j]])
+            earlier = jnp.where(is_second, sp, sm)
+            latter = jnp.where(is_second, sm, sp)
+            d_latter = jnp.where(is_second, d_mine[mine[j]][0:1], d_part[mine[j]][0:1])
+            chip_s = d_latter * earlier + latter
+            h_mine[j] = chip_s
+            c_send[j] = chip_s.astype(BF16)
+
+
+        @pl.when(z == 0)
+        def _():
+            for j in range(2):
+                t_send[j] = c_send[j]
+
+    else:
+        for j in range(2):
+            pair[1 + j].wait_recv()
+
+    @pl.when(is_second)
+    def _():
+        lax.fori_loop(0, 1, chunks, 0)
+
+    if chain:
+
+        @pl.when(early)
+        def _():
+            pl.semaphore_wait(ready.at[0], 1)
+            for copy in ring:
+                copy.start()
+
+        @pl.when(z == 0)
+        def _():
+            pl.semaphore_wait(ready.at[1], 1)
+            for copy in far:
+                copy.start()
+
+    @pl.when(is_second)
+    def _():
+        lax.fori_loop(1, cut, chunks, 0)
+
 
     if chain:
 
@@ -449,16 +463,6 @@
         copy.wait()
     pair[3].wait_recv()
     pair[4].wait_recv()
-    for copy in pair:
-        copy.wait_send()
-    if chain:
-
-        @pl.when(feeds[1])
-        def _():
-            for copy in ring:
-                copy.wait_send()
-
-
     def entering(inc, h):
         second = d_part[h][0:1] * inc + s_part[h]
         return jnp.where(is_second, second, inc).astype(BF16)
@@ -530,15 +534,6 @@
         else:
             inc = jnp.zeros((128, 128), F32)
         hb[other, :, j * 128 : (j + 1) * 128] = entering(inc, other * 2 + j)
-    for copy in back:
-        copy.wait_send()
-    if chain:
-
-        @pl.when(feeds[2])
-        def _():
-            for copy in far:
-                copy.wait_send()
-
     sends = []
     order = sorted(range(1, xn), key=lambda i: -min(i, xn - i))
     for i in order:
@@ -622,22 +617,26 @@
             for j in range(2):
                 hs = slice((h + j) * 128, (h + j + 1) * 128)
                 val = g_s[h // 2, here, j * 128 : (j + 1) * 128].astype(F32) + lift[:, j * 128 : (j + 1) * 128]
-                out_s[here, hs] = (val * scl).astype(BF16)
-        copy = pltpu.make_async_copy(
-            out_s.at[here, :], out_hbm.at[here, :], out_sem.at[q]
-        )
-        copy.start()
-        return copy
-
-    outs = [finish(mx)]
+                out_ref[here, hs] = (val * scl).astype(BF16)
+
+    finish(mx)
     for i in order[::-1]:
         q = lax.rem(mx + i, xn)
         arrived(lbuf.at[q], rgx_sem.at[q])
-        outs.append(finish(q))
-    for copy in sends:
+        finish(q)
+    for copy in pair + back + sends:
         copy.wait_send()
-    for copy in outs:
-        copy.wait()
+    if chain:
+
+        @pl.when(feeds[1])
+        def _():
+            for copy in ring:
+                copy.wait_send()
+
+        @pl.when(feeds[2])
+        def _():
+            for copy in far:
+                copy.wait_send()
 
 
 def per_device(seq_n, xn, yn, x_in, z_gate, b_input, c_input, dt_raw, a_log, d_skip, norm_gain,
@@ -667,7 +666,6 @@
         vm((2, tok, half), F32),
         vm((2, tok, half), F32),
         vm((2, tok, half), BF16),
-        vm((tok, feat), BF16),
         vm((tok, L), F32),
         vm((tok, L), F32),
         vm((nc * nh, L), F32),
@@ -704,7 +702,6 @@
         vm((yn, nc, L), F32),
         vm((tok, L), F32),
         dma((39,)),
-        dma((xn,)),
         dma((12,)),
         dma((12,)),
         dma((xn,)),
@@ -726,7 +723,7 @@
         functools.partial(kernel_body, seq_n, xn, yn),
         out_shape=jax.ShapeDtypeStruct((tok, feat), BF16),
         in_specs=[hbm] * 12,
-        out_specs=pl.BlockSpec(memory_space=pl.ANY),
+        out_specs=pl.BlockSpec(memory_space=pltpu.VMEM),
         scratch_shapes=scratch,
         compiler_params=pltpu.CompilerParams(
             collective_id=0, has_side_effects=True, vmem_limit_bytes=40 * 1024 * 1024

time: 41 us -> 41.1 us (level)
  no operation moved by 1% of the time
where the time goes in v4:
time: 41.1 us; the launch traced here: 40.9 us
  Pallas kernels  39.9 us (97%)
  local copies, waits for them, and re-layouts  0.97 us (2%)
    pallas_call x1, Pallas kernels, per_device(): call(*[pltpu.with_memory_space_constraint(v, pltpu.HBM) for v in operands])  39.9 us
    unnamed x1, local copies, waits for them, and re-layouts  0.97 us

profile of v4, /device:TPU:384, one launch (start us, length us, event | category | flops | bytes accessed | tf_op | source)
XLA Modules:
  0.0 40.9 jit_solution(8171448042530843454)
XLA Ops:
  0.0 39.9 %shard_map.118 = bf16[1024,512]{1,0:T(8,128)(2,1)S(1)} custom-call(s32[6]{0:T(128)} %doc_len_hbm.1, s32[6]{0:T(128)} %doc_lang_hbm.1, f32[4]{0:T(128)} %a_log_hbm.1, f32[4]{0:T(128)} %d_skip_hbm.1, f32[4,1024]{1,0:T(4,128)} %dt_hbm.1, f32[1,512]{1,0:T(1,128)} %bitcast.7, bf16[1024,512]{1,0:T(8,128)(2,1)} %x_hbm.1, bf16[1024,512]{1,0:T(8,128)(2,1)} %z_hbm.1, ...), custom_call_target="tpu_custom_call" | custom-call | tf_op jit(solution)/shard_map/pallas_call | solution.py:746
  39.9 1.0 %copy.14 = bf16[1024,512]{1,0:T(8,128)(2,1)} copy(bf16[1024,512]{1,0:T(8,128)(2,1)S(1)} %shard_map.118) | data formatting | bytes 2097152
